TPU v7x, 512 devices: a whole 4x4x16 slice. The times are simulated.
512 devices in a mesh: ga: 64 (over z, x), band: 8 (over y, core).
Axes of the slice: x: 4, y: 4, z: 16, core: 2. Of those that a mesh axis runs over, the one named last changes fastest.
Arguments:
- orbitals: bfloat16 [8, 2, 2048, 192], P(None, None, ('ga', 'band')), may hold values from -6 to 6
- projectors: bfloat16 [512, 2, 2048, 192], P(None, None, ('ga', 'band')), may hold values from -0.046875 to 0.046875
- potential: float32 [192, 192, 192], P('ga'), may hold values from -2 to 0.5
- couplings: float32 [512, 512], replicated, may hold values from -3 to 3
- atom_index: int32 [512], replicated, may hold values from 0 to 63
- column_site: int32 [2048], replicated, may hold values from 0 to 36863, as said below
- column_count: int32 [64], replicated, may hold values from 8 to 32, as said below
Outputs:
- applied: float32 [8, 2, 2048, 192], P(None, None, ('ga', 'band'))
Inputs may be any that keep to these rules, and one draw needn't show every extreme that they name: `column_site`: distinct positions kx * 192 + ky in the 192 x 192 plane of frequencies. `column_count`: the slot b * 4 + j of band index b in a ga block is used where it lies below that block's count; some ga block has all 32 slots used.
All inputs are finite; a program needn't handle non-finite values.
Results may differ from a plain program's by a relative error of at most 0.0027.
Values may be sent and summed in bfloat16 or wider, within the bound.
A program may use at most 128 MiB of HBM per device.

v0:
```python
import math

import jax
import jax.numpy as jnp
import ml_dtypes
import numpy as np
from jax import lax
from jax.experimental import pallas as pl
from jax.experimental.pallas import tpu as pltpu
from jax.sharding import PartitionSpec as P

MESH = pl.DeviceIdType.MESH
F32 = jnp.float32
BF16 = jnp.bfloat16
GRID = 192
ZN, XN, BN = 16, 4, 8


def split_host(table):
    high = table.astype(ml_dtypes.bfloat16)
    low = (table - high.astype(np.float64)).astype(ml_dtypes.bfloat16)
    return high, low


def make_tables():
    points = np.arange(GRID)
    phases = (points[:, None] * points[None, :] % GRID) * (2.0 * math.pi / GRID)
    order = np.arange(GRID).reshape(2, 4, 3, 8)
    hi, mid, sub, lo = np.meshgrid(np.arange(2), np.arange(4), np.arange(3), np.arange(8), indexing="ij")
    order = (12 * (8 * hi + lo) + 3 * mid + sub).reshape(-1)
    out = []
    for angles in (phases, phases[:, order]):
        cos_h, cos_l = split_host(np.cos(angles))
        sin_h, sin_l = split_host(np.sin(angles))
        out.append(np.concatenate([cos_h, sin_h, cos_l, sin_l], axis=0))
    return out


def dot(left, right):
    return lax.dot_general(left, right, (((1,), (0,)), ((), ())), preferred_element_type=F32)


def dot_nt(left, right):
    return lax.dot_general(left, right, (((1,), (1,)), ((), ())), preferred_element_type=F32)


def split(value):
    high = value.astype(BF16)
    return high, (value - high.astype(F32)).astype(BF16)


def kernel(
    count_ref, site_ref, atom_ref, orb_ref, proj_ref, pot_ref, coup_ref, plane_ref, ztab_ref, out_ref,
    coef, coef_rot, send_b, recv_b, send_pb, recv_pb, turn, send_x, recv_x, send_px, recv_px,
    send_z, recv_z, send_pz, recv_pz, columns, picks_x, picks_y, weights, grid_sum, grid_back,
    coupled_h, coupled_l, back_z, got_z, back_x, got_x, back_px, got_px, back_b, got_b, back_pb, got_pb,
    pairs, wide, sems,
):
    block = lax.axis_index("ga")
    band = lax.axis_index("band")
    zz = block // XN
    xx = block % XN

    def on_band(d):
        return (block, (band + d) % BN), (band + d) % BN

    def on_x(d):
        return (zz * XN + (xx + d) % XN, band), (xx + d) % XN

    def on_z(d):
        return (((zz + d) % ZN) * XN + xx, band), (zz + d) % ZN

    def exchange(first_sem, size, where, source, target):
        def copy(d):
            device, index = where(d)
            return pltpu.make_async_remote_copy(
                src_ref=source(index),
                dst_ref=target,
                send_sem=sems.at[0, first_sem + d],
                recv_sem=sems.at[1, first_sem + d],
                device_id=device,
                device_id_type=MESH,
            )

        def start():
            @pl.loop(1, size)
            def _(d):
                copy(d).start()

        def wait():
            @pl.loop(1, size)
            def _(d):
                copy(d).wait()

        return start, wait

    def rows8(ref, index):
        return ref.at[pl.ds(pl.multiple_of(index * 8, 8), 8)]

    cols_b = exchange(0, BN, on_band, lambda i: send_b.at[i], recv_b.at[band])
    proj_b = exchange(8, BN, on_band, lambda i: rows8(send_pb, i), rows8(recv_pb, band))
    cols_x = exchange(16, XN, on_x, lambda i: send_x.at[i], recv_x.at[xx])
    proj_x = exchange(20, XN, on_x, lambda i: send_px, rows8(recv_px, xx))
    cols_z = exchange(24, ZN, on_z, lambda i: rows8(send_z, i), rows8(recv_z, zz))
    proj_z = exchange(40, ZN, on_z, lambda i: send_pz, rows8(recv_pz, zz))
    sums_x = exchange(56, XN, on_x, lambda i: back_px, rows8(got_px, xx))
    sums_b = exchange(60, BN, on_band, lambda i: back_pb, rows8(got_pb, band))
    home_z = exchange(68, ZN, on_z, lambda i: rows8(back_z, i), rows8(got_z, zz))
    home_x = exchange(84, XN, on_x, lambda i: back_x.at[i], got_x.at[xx])
    home_b = exchange(88, BN, on_band, lambda i: back_b.at[i], got_b.at[band])

    barrier = pltpu.get_barrier_semaphore()
    for size, where in ((ZN, on_z), (XN, on_x), (BN, on_band)):

        @pl.loop(1, size)
        def _(d, where=where):
            pl.semaphore_signal(barrier, inc=1, device_id=where(d)[0], device_id_type=MESH)

    used = count_ref[block]
    row64 = lax.broadcasted_iota(jnp.int32, (64, GRID), 0)
    active = jnp.where(band * 4 + row64 % 4 < used, 1.0, 0.0).astype(F32)
    for n in range(8):
        real = orb_ref[2 * n].astype(F32)
        imag = orb_ref[2 * n + 1].astype(F32)
        coef[8 * n : 8 * n + 4, :] = real
        coef[8 * n + 4 : 8 * n + 8, :] = imag
        coef_rot[8 * n : 8 * n + 4, :] = -imag
        coef_rot[8 * n + 4 : 8 * n + 8, :] = real
    coef[...] = coef[...] * active
    coef_rot[...] = coef_rot[...] * active
    plain = coef[...].astype(BF16)
    rotated = coef_rot[...].astype(BF16)
    along_z = (
        dot(plain, ztab_ref[0:192, :])
        + dot(plain, ztab_ref[384:576, :])
        + dot(rotated, ztab_ref[192:384, :])
        + dot(rotated, ztab_ref[576:768, :])
    )
    send_b[...] = along_z.reshape(8, 8, GRID)

    wide[0, 0:64, :] = coef[:, 0:128]
    wide[1, 0:64, 0:64] = coef[:, 128:192]
    wide[0, 64:128, :] = -coef_rot[:, 0:128]
    wide[1, 64:128, 0:64] = -coef_rot[:, 128:192]

    def slot_rows(start):
        halves = [wide[h, pl.ds(start, 16, stride=4), :] for h in range(2)]
        return jnp.concatenate(halves, axis=1)[:, 0:GRID]

    partial = jnp.zeros((16, 512), F32)
    for slot in range(4):
        left = slot_rows(slot).astype(BF16)
        right = slot_rows(64 + slot).astype(BF16)
        partial += dot(left, proj_ref[slot * 192 : (slot + 1) * 192, :])
        partial += dot(right, proj_ref[(slot + 4) * 192 : (slot + 5) * 192, :])
    for part in range(4):
        send_pb[pl.ds(part, 16, stride=4), :] = partial[:, part * 128 : (part + 1) * 128]

    pl.semaphore_wait(barrier, ZN + XN + BN - 3)
    cols_b[0]()
    proj_b[0]()

    @pl.loop(0, ZN)
    def _(s):
        site = site_ref[pl.ds(s, 1), :]
        kx = (site * 43691) >> 23
        ky = site - kx * 192
        rows = lax.broadcasted_iota(jnp.int32, (GRID, 128), 0)
        lanes = pl.ds(pl.multiple_of(s * 128, 128), 128)
        picks_x[:, lanes] = jnp.where(rows == kx, 1.0, 0.0).astype(BF16)
        picks_y[:, lanes] = jnp.where(rows == ky, 1.0, 0.0).astype(BF16)

    recv_b[pl.ds(band, 1)] = send_b[pl.ds(band, 1)]
    cols_b[1]()
    turn[...] = jnp.zeros_like(turn)
    for b in range(8):
        for c in range(2):
            turn[c * 32 + b * 4 : c * 32 + b * 4 + 4, 0:GRID] = recv_b[b, 4 * c : 4 * c + 4, :]
    turned = turn[...].T
    lane96 = lax.broadcasted_iota(jnp.int32, (96, 128), 1)
    joined = jnp.where(lane96 < 64, turned[0:96], pltpu.roll(turned[96:192], 64, 1))
    send_x[...] = joined.reshape(4, 24, 128)
    cols_x[0]()

    rows8(recv_pb, band)[...] = rows8(send_pb, band)[...]
    proj_b[1]()
    total = recv_pb[0:8, :]
    for b in range(1, 8):
        total += recv_pb[8 * b : 8 * b + 8, :]
    send_px[...] = total
    rows8(recv_px, xx)[...] = total
    proj_x[0]()

    recv_x[pl.ds(xx, 1)] = send_x[pl.ds(xx, 1)]
    cols_x[1]()
    lane24 = lax.broadcasted_iota(jnp.int32, (24, 128), 1)
    for x_lo in range(2):
        low = recv_x[x_lo]
        high = recv_x[x_lo + 2]
        for z_hi in range(2):
            if z_hi == 0:
                pair = jnp.where(lane24 < 64, low, pltpu.roll(high, 64, 1))
            else:
                pair = jnp.where(lane24 < 64, pltpu.roll(low, 64, 1), high)
            for zi in range(3):
                send_z[pl.ds(z_hi * 64 + x_lo * 3 + zi, 8, stride=8), :] = pair[8 * zi : 8 * zi + 8]
                if x_lo == 0 and zi < 2:
                    send_z[pl.ds(z_hi * 64 + 6 + zi, 8, stride=8), :] = jnp.zeros((8, 128), F32)
    cols_z[0]()

    proj_x[1]()
    total = recv_px[0:8, :]
    for x in range(1, 4):
        total += recv_px[8 * x : 8 * x + 8, :]
    grow = lax.broadcasted_iota(jnp.int32, (8, 128), 0)
    mine_r = jnp.sum(jnp.where(grow == xx, total, 0.0), axis=0, keepdims=True)
    mine_i = jnp.sum(jnp.where(grow == xx + 4, total, 0.0), axis=0, keepdims=True)
    mine = jnp.where(grow == 0, mine_r, jnp.where(grow == 1, mine_i, 0.0))
    send_pz[...] = mine
    rows8(recv_pz, zz)[...] = mine
    proj_z[0]()

    atoms = lax.broadcasted_iota(jnp.int32, (64, 128), 0)
    marks = jnp.concatenate(
        [jnp.where(atoms == atom_ref[q : q + 1, :], 1.0, 0.0).astype(F32) for q in range(4)], axis=1
    )
    same = dot(marks.T.astype(BF16), marks.astype(BF16))
    coupled = jnp.where(same > 0.5, coup_ref[...], 0.0)
    part_h, part_l = split(coupled)
    coupled_h[...] = part_h
    coupled_l[...] = part_l

    rows8(recv_z, zz)[...] = rows8(send_z, zz)[...]
    cols_z[1]()
    lane16 = lax.broadcasted_iota(jnp.int32, (16, 128), 1)
    even = (lane16 // 32) % 2 == 0
    for zi in range(3):
        first = recv_z[pl.ds(zi, 16, stride=8), :]
        second = recv_z[pl.ds(zi + 3, 16, stride=8), :]
        columns[zi * 32 : zi * 32 + 16, :] = jnp.where(even, first, pltpu.roll(second, 32, 1))
        columns[zi * 32 + 16 : zi * 32 + 32, :] = jnp.where(even, pltpu.roll(first, 96, 1), second)

    grid_sum[...] = jnp.zeros_like(grid_sum)

    @pl.loop(0, 8)
    def _(t):
        for h in range(2):
            s = 2 * t + h
            spots = picks_x[:, pl.ds(pl.multiple_of(s * 128, 128), 128)]
            for i in range(6):
                value = columns[pl.ds(i * 16 + s, 1), :]
                spread = jnp.broadcast_to(value, (GRID, 128)).astype(BF16)
                weights[i * 192 : (i + 1) * 192, h * 128 : (h + 1) * 128] = spots * spread
        grid_sum[...] += dot_nt(weights[...], picks_y[:, pl.ds(pl.multiple_of(t * 256, 256), 256)])

    proj_z[1]()
    total = recv_pz[0:8, :]
    for z in range(1, 16):
        total += recv_pz[8 * z : 8 * z + 8, :]
    back_px[...] = total
    rows8(got_px, xx)[...] = total
    sums_x[0]()

    table = plane_ref[...]
    cos_h, sin_h, cos_l, sin_l = (table[192 * i : 192 * (i + 1)] for i in range(4))
    scale = 1.0 / float(GRID**3)

    def along_x(value):
        high, low = split(value)
        one = dot(table, high)
        two = dot(table[0:384], low)
        both = one[0:384] + one[384:768] + two
        return both[0:192], both[192:384]

    @pl.loop(0, 3)
    def _(zi):
        rows = pl.ds(pl.multiple_of(zi * 384, 384), 384)
        start = grid_sum[rows, :].astype(BF16)
        by_cos = dot(start, cos_h) + dot(start, cos_l)
        by_sin = dot(start, sin_h) + dot(start, sin_l)
        real_c, real_s = along_x(by_cos[0:192] - by_sin[192:384])
        imag_c, imag_s = along_x(by_sin[0:192] + by_cos[192:384])
        field = pot_ref[zi] * scale
        real_c, real_s, imag_c, imag_s = along_x((real_c - imag_s) * field) + along_x((real_s + imag_c) * field)
        high, low = split(jnp.concatenate([real_c + imag_s, imag_c - real_s], axis=0))
        by_cos = dot(high, cos_h) + dot(high, cos_l) + dot(low, cos_h)
        by_sin = dot(high, sin_h) + dot(high, sin_l) + dot(low, sin_h)
        grid_back[rows, :] = jnp.concatenate(
            [by_cos[0:192] + by_sin[192:384], by_cos[192:384] - by_sin[0:192]], axis=0
        ).astype(BF16)

    sums_x[1]()
    for x in range(4):
        for c in range(2):
            back_pb[c * 4 + x : c * 4 + x + 1, :] = got_px[8 * x + c : 8 * x + c + 1, :]
    rows8(got_pb, band)[...] = back_pb[...]
    sums_b[0]()

    @pl.loop(0, 8)
    def _(t):
        lanes = pl.ds(pl.multiple_of(t * 256, 256), 256)
        picked = dot(grid_back[...], picks_y[:, lanes])
        spots = picks_x[:, lanes].astype(F32)
        for i in range(6):
            value = jnp.sum(picked[i * 192 : (i + 1) * 192] * spots, axis=0, keepdims=True)
            for h in range(2):
                columns[pl.ds(i * 16 + 2 * t + h, 1), :] = value[:, h * 128 : (h + 1) * 128]

    for zi in range(3):
        real = columns[zi * 32 : zi * 32 + 16, :]
        imag = columns[zi * 32 + 16 : zi * 32 + 32, :]
        back_z[pl.ds(zi, 16, stride=8), :] = jnp.where(even, real, pltpu.roll(imag, 32, 1))
        back_z[pl.ds(zi + 3, 16, stride=8), :] = jnp.where(even, pltpu.roll(real, 96, 1), imag)
    for row in (6, 7):
        back_z[pl.ds(row, 16, stride=8), :] = jnp.zeros((16, 128), F32)
    home_z[0]()

    sums_b[1]()
    for part in range(4):
        lanes = slice(part * 128, (part + 1) * 128)
        real = got_pb[pl.ds(part, 8, stride=8), :]
        imag = got_pb[pl.ds(part + 4, 8, stride=8), :]
        pairs[part, pl.ds(0, 8, stride=2), :] = real
        pairs[part, pl.ds(1, 8, stride=2), :] = imag
        pairs[part, pl.ds(16, 8, stride=2), :] = -imag
        pairs[part, pl.ds(17, 8, stride=2), :] = real
    high, low = split(jnp.concatenate([pairs[part] for part in range(4)], axis=1))
    weighted = dot_nt(high, coupled_h[...]) + dot_nt(high, coupled_l[...]) + dot_nt(low, coupled_h[...])
    weighted = weighted.astype(BF16)
    for slot in range(4):
        mixed = dot_nt(weighted[0:16], proj_ref[slot * 192 : (slot + 1) * 192, :]) + dot_nt(
            weighted[16:32], proj_ref[(slot + 4) * 192 : (slot + 5) * 192, :]
        )
        wide[0, pl.ds(slot, 16, stride=4), :] = mixed[:, 0:128]
        wide[1, pl.ds(slot, 16, stride=4), :] = jnp.concatenate([mixed[:, 128:192], jnp.zeros((16, 64), F32)], axis=1)

    rows8(got_z, zz)[...] = rows8(back_z, zz)[...]
    home_z[1]()
    lane8 = lax.broadcasted_iota(jnp.int32, (8, 128), 1)
    for x_lo in range(2):
        for zi in range(3):
            first = got_z[pl.ds(x_lo * 3 + zi, 8, stride=8), :]
            second = got_z[pl.ds(64 + x_lo * 3 + zi, 8, stride=8), :]
            back_x[x_lo, 8 * zi : 8 * zi + 8, :] = jnp.where(lane8 < 64, first, pltpu.roll(second, 64, 1))
            back_x[x_lo + 2, 8 * zi : 8 * zi + 8, :] = jnp.where(lane8 < 64, pltpu.roll(first, 64, 1), second)
    home_x[0]()
    got_x[pl.ds(xx, 1)] = back_x[pl.ds(xx, 1)]
    home_x[1]()
    joined = got_x[...].reshape(96, 128)
    turned = jnp.concatenate([joined, pltpu.roll(joined, 64, 1), jnp.zeros((64, 128), F32)], axis=0).T
    for b in range(8):
        for c in range(2):
            back_b[b, 4 * c : 4 * c + 4, :] = turned[c * 32 + b * 4 : c * 32 + b * 4 + 4, 0:GRID]
    home_b[0]()
    got_b[pl.ds(band, 1)] = back_b[pl.ds(band, 1)]
    home_b[1]()
    for n in range(8):
        coef[8 * n : 8 * n + 4, :] = got_b[n, 0:4, :]
        coef[8 * n + 4 : 8 * n + 8, :] = got_b[n, 4:8, :]
        coef_rot[8 * n : 8 * n + 4, :] = got_b[n, 4:8, :]
        coef_rot[8 * n + 4 : 8 * n + 8, :] = -got_b[n, 0:4, :]
    plain_h, plain_l = split(coef[...])
    rotated_h, rotated_l = split(coef_rot[...])
    local = (
        dot_nt(plain_h, ztab_ref[0:192, :])
        + dot_nt(plain_h, ztab_ref[384:576, :])
        + dot_nt(plain_l, ztab_ref[0:192, :])
        + dot_nt(rotated_h, ztab_ref[192:384, :])
        + dot_nt(rotated_h, ztab_ref[576:768, :])
        + dot_nt(rotated_l, ztab_ref[192:384, :])
    )
    projected = jnp.concatenate([wide[0, 0:64, :], wide[1, 0:64, :]], axis=1)[:, 0:GRID]
    result = (local + projected) * active
    for i in range(16):
        out_ref[i] = result[4 * i : 4 * i + 4, :]


def on_device(orbitals, projectors, potential, couplings, atom_index, column_site, column_count):
    plane, ztab = (jnp.asarray(t) for t in make_tables())
    vmem = pl.BlockSpec(memory_space=pltpu.VMEM)
    smem = pl.BlockSpec(memory_space=pltpu.SMEM)
    flat = projectors.transpose(1, 2, 3, 0).reshape(8 * GRID, 512)
    scratch = lambda *shape: pltpu.VMEM(shape, F32)
    out = pl.pallas_call(
        kernel,
        out_shape=jax.ShapeDtypeStruct((16, 4, GRID), F32),
        in_specs=[smem] + [vmem] * 8,
        out_specs=vmem,
        scratch_shapes=[
            scratch(64, GRID),
            scratch(64, GRID),
            scratch(8, 8, GRID),
            scratch(8, 8, GRID),
            scratch(64, 128),
            scratch(64, 128),
            scratch(128, 256),
            scratch(4, 24, 128),
            scratch(4, 24, 128),
            scratch(8, 128),
            scratch(32, 128),
            scratch(128, 128),
            scratch(128, 128),
            scratch(8, 128),
            scratch(128, 128),
            scratch(96, 128),
            pltpu.VMEM((GRID, 2048), BF16),
            pltpu.VMEM((GRID, 2048), BF16),
            pltpu.VMEM((1152, 256), BF16),
            scratch(1152, GRID),
            pltpu.VMEM((1152, GRID), BF16),
            pltpu.VMEM((512, 512), BF16),
            pltpu.VMEM((512, 512), BF16),
            scratch(128, 128),
            scratch(128, 128),
            scratch(4, 24, 128),
            scratch(4, 24, 128),
            scratch(8, 128),
            scratch(32, 128),
            scratch(8, 8, GRID),
            scratch(8, 8, GRID),
            scratch(8, 128),
            scratch(64, 128),
            scratch(4, 32, 128),
            scratch(2, 128, 128),
            pltpu.SemaphoreType.DMA((2, 96)),
        ],
        compiler_params=pltpu.CompilerParams(
            collective_id=0, has_side_effects=True, vmem_limit_bytes=48 * 1024 * 1024
        ),
    )(
        column_count,
        column_site.reshape(16, 128),
        atom_index.reshape(4, 128),
        orbitals.reshape(16, 4, GRID),
        flat,
        potential,
        couplings,
        plane,
        ztab,
    )
    return out.reshape(8, 2, 4, GRID)


def solution(mesh):
    return jax.shard_map(
        on_device,
        mesh=mesh,
        in_specs=(
            P(None, None, ("ga", "band"), None),
            P(None, None, ("ga", "band"), None),
            P("ga", None, None),
            P(),
            P(),
            P(),
            P(),
        ),
        out_specs=P(None, None, ("ga", "band"), None),
        check_vma=False,
    )
```

profile of v0, /device:TPU:1, one launch (start us, length us, event | category | flops | bytes accessed | tf_op | source)
XLA Modules:
  0.0 74.9 jit_solution(6852044885788148461)
XLA Ops:
  0.0 0.0 copy-start
  0.0 1.4 %copy-done = bf16[512,2,4,192]{0,3,2,1:T(8,128)(2,1)S(1)} copy-done((bf16[512,2,4,192]{0,3,2,1:T(8,128)(2,1)S(1)}, bf16[512,2,4,192]{0,3,2,1:T(8,128)(2,1)}, u32[]{:S(2)}) %copy-start) | copy-done | bytes 1572888
  1.4 0.0 copy-start.1
  1.4 1.2 %copy-done.1 = f32[512,512]{1,0:T(8,128)S(1)} copy-done((f32[512,512]{1,0:T(8,128)S(1)}, f32[512,512]{1,0:T(8,128)}, u32[]{:S(2)}) %copy-start.1) | copy-done | bytes 1048600
  2.6 0.0 copy-start.2
  2.6 1.1 %copy-done.2 = f32[3,192,192]{2,1,0:T(8,128)S(1)} copy-done((f32[3,192,192]{2,1,0:T(8,128)S(1)}, f32[3,192,192]{2,1,0:T(8,128)}, u32[]{:S(2)}) %copy-start.2) | copy-done | bytes 442392
  3.7 0.0 copy-start.3
  3.7 1.0 %copy-done.3 = bf16[768,192]{1,0:T(8,128)(2,1)S(1)} copy-done((bf16[768,192]{1,0:T(8,128)(2,1)S(1)}, bf16[768,192]{1,0:T(8,128)(2,1)}, u32[]{:S(2)}) %copy-start.3) | copy-done | bytes 294936
  4.7 0.0 copy-start.4
  4.7 1.0 %copy-done.4 = bf16[768,192]{1,0:T(8,128)(2,1)S(1)} copy-done((bf16[768,192]{1,0:T(8,128)(2,1)S(1)}, bf16[768,192]{1,0:T(8,128)(2,1)}, u32[]{:S(2)}) %copy-start.4) | copy-done | bytes 294936
  5.7 0.0 copy-start.5
  5.7 0.8 %copy-done.5 = bf16[8,2,4,192]{3,2,1,0:T(4,128)(2,1)S(1)} copy-done((bf16[8,2,4,192]{3,2,1,0:T(4,128)(2,1)S(1)}, bf16[8,2,4,192]{3,2,1,0:T(4,128)(2,1)}, u32[]{:S(2)}) %copy-start.5) | copy-done | bytes 24600
  6.5 0.0 copy-start.6
  6.5 0.7 copy-done.6
  7.1 0.0 copy-start.7
  7.1 0.7 copy-done.7
  7.8 0.0 copy-start.8
  7.8 0.7 copy-done.8
  8.5 65.8 %shard_map.91 = f32[16,4,192]{2,1,0:T(4,128)S(1)} custom-call(s32[64]{0:T(128)S(1)} %copy-done.8, s32[16,128]{1,0:T(8,128)S(1)} %bitcast.10, s32[4,128]{1,0:T(4,128)S(1)} %bitcast.11, bf16[16,4,192]{2,1,0:T(4,128)(2,1)S(1)} %bitcast.9, bf16[1536,512]{1,0:T(8,128)(2,1)S(1)} %bitcast.7, f32[3,192,192]{2,1,0:T(8,128)S(1)} %copy-done.2, ...), custom_call_target="tpu_custom_call" | custom-call | tf_op jit(solution)/shard_map/pallas_call | solution.py:384
  74.3 0.6 copy.11
Async XLA Ops:
  0.0 1.4 %copy-start = (bf16[512,2,4,192]{0,3,2,1:T(8,128)(2,1)S(1)}, bf16[512,2,4,192]{0,3,2,1:T(8,128)(2,1)}, u32[]{:S(2)}) copy-start(bf16[512,2,4,192]{0,3,2,1:T(8,128)(2,1)} %param.10) | copy-start | bytes 4718596
  1.4 1.2 %copy-start.1 = (f32[512,512]{1,0:T(8,128)S(1)}, f32[512,512]{1,0:T(8,128)}, u32[]{:S(2)}) copy-start(f32[512,512]{1,0:T(8,128)} %coup_ref.1) | copy-start | bytes 3145732
  2.6 1.1 %copy-start.2 = (f32[3,192,192]{2,1,0:T(8,128)S(1)}, f32[3,192,192]{2,1,0:T(8,128)}, u32[]{:S(2)}) copy-start(f32[3,192,192]{2,1,0:T(8,128)} %pot_ref.1) | copy-start | bytes 1327108
  3.7 1.0 %copy-start.3 = (bf16[768,192]{1,0:T(8,128)(2,1)S(1)}, bf16[768,192]{1,0:T(8,128)(2,1)}, u32[]{:S(2)}) copy-start(bf16[768,192]{1,0:T(8,128)(2,1)} %constant.5.clone.ztab_ref) | copy-start | bytes 884740
  4.7 1.0 %copy-start.4 = (bf16[768,192]{1,0:T(8,128)(2,1)S(1)}, bf16[768,192]{1,0:T(8,128)(2,1)}, u32[]{:S(2)}) copy-start(bf16[768,192]{1,0:T(8,128)(2,1)} %constant.4.clone.plane_ref) | copy-start | bytes 884740
  5.7 0.8 %copy-start.5 = (bf16[8,2,4,192]{3,2,1,0:T(4,128)(2,1)S(1)}, bf16[8,2,4,192]{3,2,1,0:T(4,128)(2,1)}, u32[]{:S(2)}) copy-start(bf16[8,2,4,192]{3,2,1,0:T(4,128)(2,1)} %param.9) | copy-start | bytes 73732
  6.5 0.7 copy-start.6
  7.1 0.7 copy-start.7
  7.8 0.7 copy-start.8
where the time goes:
time: 75.4 us; the launch traced here: 74.9 us
  Pallas kernels  65.8 us (87%)
  local copies, waits for them, and re-layouts  9.11 us (12%)
    pallas_call x1, Pallas kernels, on_device(): pl.pallas_call(kernel, out_shape=jax.ShapeDtypeStruct((16, 4, GRID), F32)...  65.8 us
    unnamed x19, local copies, waits for them, and re-layouts  9.11 us

commit v1 on v0

v1 whole, which is shorter than its diff:
```python
import math

import jax
import jax.numpy as jnp
import ml_dtypes
import numpy as np
from jax import lax
from jax.experimental import pallas as pl
from jax.experimental.pallas import tpu as pltpu
from jax.sharding import PartitionSpec as P

MESH = pl.DeviceIdType.MESH
F32 = jnp.float32
BF16 = jnp.bfloat16
GRID = 192
ZN, XN, BN = 16, 4, 8


def split_host(table):
    high = table.astype(ml_dtypes.bfloat16)
    low = (table - high.astype(np.float64)).astype(ml_dtypes.bfloat16)
    return high, low


def make_tables():
    points = np.arange(GRID)
    phases = (points[:, None] * points[None, :] % GRID) * (2.0 * math.pi / GRID)
    lanes = np.full((XN, 128), -1)
    for x in range(XN):
        for sub in range(3):
            lanes[x, 16 * sub : 16 * sub + 16] = 12 * np.arange(ZN) + 3 * x + sub
    lanes = lanes.reshape(-1)
    out = []
    for pick in (points, lanes):
        angles = phases[:, pick]
        cos_h, cos_l = split_host(np.where(pick < 0, 0.0, np.cos(angles)))
        sin_h, sin_l = split_host(np.where(pick < 0, 0.0, np.sin(angles)))
        out.append(np.concatenate([cos_h, sin_h, cos_l, sin_l], axis=0))
    return out


def dot(left, right):
    return lax.dot_general(left, right, (((1,), (0,)), ((), ())), preferred_element_type=F32)


def dot_nt(left, right):
    return lax.dot_general(left, right, (((1,), (1,)), ((), ())), preferred_element_type=F32)


def split(value):
    high = value.astype(BF16)
    return high, (value - high.astype(F32)).astype(BF16)


def kernel(
    count_ref, site_hbm, atom_hbm, orb_hbm, proj_hbm, pot_hbm, coup_hbm, plane_hbm, ztab_hbm, out_ref,
    site_ref, atom_ref, orb_ref, proj_ref, pot_ref, coup_ref, plane_ref, ztab_ref,
    coef, coef_rot, wide, send_b, recv_b, send_pb, recv_pb, turn, stage, send_z, recv_z, send_pz, recv_pz,
    picks_x, picks_y, weights, grid_sum, grid_back, coupled_h, coupled_l, found, back_z, got_z,
    back_b, got_b, back_pb, got_pb, pairs, sems, load_sems,
):
    block = lax.axis_index("ga")
    band = lax.axis_index("band")
    zz = lax.div(block, XN)
    xx = lax.rem(block, XN)
    me = xx * BN + band

    arrays = (
        (orb_hbm, orb_ref), (ztab_hbm, ztab_ref), (proj_hbm, proj_ref), (site_hbm, site_ref),
        (atom_hbm, atom_ref), (coup_hbm, coup_ref), (plane_hbm, plane_ref), (pot_hbm, pot_ref),
    )
    loads = [pltpu.make_async_copy(far, near, load_sems.at[i]) for i, (far, near) in enumerate(arrays)]
    orb_in, ztab_in, proj_in, site_in, atom_in, coup_in, plane_in, pot_in = loads

    def on_plane(d):
        index = lax.rem(me + d, XN * BN)
        return (zz * XN + lax.div(index, BN), lax.rem(index, BN)), index

    def on_z(d):
        index = lax.rem(zz + d, ZN)
        return (index * XN + xx, band), index

    def exchange(first_sem, size, where, source, target):
        def copy(d):
            device, index = where(d)
            return pltpu.make_async_remote_copy(
                src_ref=source(index),
                dst_ref=target,
                send_sem=sems.at[0, first_sem + d],
                recv_sem=sems.at[1, first_sem + d],
                device_id=device,
                device_id_type=MESH,
            )

        def start():
            @pl.loop(1, size)
            def _(d):
                copy(d).start()

        def wait():
            @pl.loop(1, size)
            def _(d):
                copy(d).wait()

        return start, wait, copy

    def rows8(ref, index):
        return ref.at[pl.ds(pl.multiple_of(index * 8, 8), 8)]

    peers = XN * BN
    cols_b = exchange(0, peers, on_plane, lambda i: send_b.at[i], recv_b.at[me])
    proj_b = exchange(32, peers, on_plane, lambda i: rows8(send_pb, i), rows8(recv_pb, me))
    cols_z = exchange(64, ZN, on_z, lambda i: send_z.at[i], recv_z.at[zz])
    proj_z = exchange(80, ZN, on_z, lambda i: send_pz, rows8(recv_pz, zz))
    sums_b = exchange(96, peers, on_plane, lambda i: back_pb, rows8(got_pb, me))
    home_z = exchange(128, ZN, on_z, lambda i: back_z.at[i], got_z.at[zz])
    home_b = exchange(144, peers, on_plane, lambda i: back_b.at[i], got_b.at[me])

    barrier = pltpu.get_barrier_semaphore()
    orb_in.start()
    ztab_in.start()

    @pl.loop(0, ZN - 1)
    def _(i):
        away = lax.rem(i + 8, ZN - 1) + 1
        pl.semaphore_signal(barrier, inc=1, device_id=on_z(away)[0], device_id_type=MESH)

    @pl.loop(1, peers)
    def _(d):
        pl.semaphore_signal(barrier, inc=1, device_id=on_plane(d)[0], device_id_type=MESH)

    for load in loads[2:]:
        load.start()

    used = count_ref[block]
    row64 = lax.broadcasted_iota(jnp.int32, (64, GRID), 0)
    active = jnp.where(band * 4 + row64 % 4 < used, 1.0, 0.0).astype(F32)
    orb_in.wait()
    for n in range(8):
        real = orb_ref[2 * n].astype(F32)
        imag = orb_ref[2 * n + 1].astype(F32)
        coef[8 * n : 8 * n + 4, :] = real
        coef[8 * n + 4 : 8 * n + 8, :] = imag
        coef_rot[8 * n : 8 * n + 4, :] = -imag
        coef_rot[8 * n + 4 : 8 * n + 8, :] = real
    coef[...] = coef[...] * active
    coef_rot[...] = coef_rot[...] * active
    plain = coef[...].astype(BF16)
    rotated = coef_rot[...].astype(BF16)
    ztab_in.wait()
    along_z = (
        dot(plain, ztab_ref[0:192, :])
        + dot(plain, ztab_ref[384:576, :])
        + dot(rotated, ztab_ref[192:384, :])
        + dot(rotated, ztab_ref[576:768, :])
    )
    for x in range(XN):
        send_b[8 * x : 8 * x + 8] = along_z[:, 128 * x : 128 * x + 128].reshape(8, 8, 128).astype(BF16)

    wide[0, 0:64, :] = coef[:, 0:128]
    wide[1, 0:64, 0:64] = coef[:, 128:192]
    wide[0, 64:128, :] = -coef_rot[:, 0:128]
    wide[1, 64:128, 0:64] = -coef_rot[:, 128:192]

    def slot_rows(start):
        parts = [
            jnp.concatenate([wide[h, pl.ds(start + 4 * c, 8, stride=8), :] for h in range(2)], axis=1)
            for c in range(2)
        ]
        return jnp.concatenate(parts, axis=0)[:, 0:GRID].astype(BF16)

    proj_in.wait()
    partial = jnp.zeros((16, 512), F32)
    for slot in range(4):
        partial += dot(slot_rows(slot), proj_ref[slot * 192 : (slot + 1) * 192, :])
        partial += dot(slot_rows(64 + slot), proj_ref[(slot + 4) * 192 : (slot + 5) * 192, :])
    send_pb[...] = jnp.zeros_like(send_pb)
    for x in range(XN):
        for c in range(2):
            send_pb[pl.ds(64 * x + c, 8, stride=8), :] = partial[8 * c : 8 * c + 8, 128 * x : 128 * x + 128]

    pl.semaphore_wait(barrier, ZN + peers - 2)
    cols_b[0]()

    stage[...] = jnp.zeros_like(stage)
    found[...] = jnp.zeros_like(found)
    grid_sum[...] = jnp.zeros_like(grid_sum)
    site_in.wait()

    def sources(t):
        return lax.rem(zz + ZN - t, ZN), lax.rem(zz + t + 1, ZN)

    @pl.loop(0, 8)
    def _(t):
        rows = lax.broadcasted_iota(jnp.int32, (GRID, 128), 0)
        for h, s in enumerate(sources(t)):
            site = site_ref[pl.ds(s, 1), :]
            kx = (site * 43691) >> 23
            ky = site - kx * 192
            lanes = pl.ds(pl.multiple_of(t * 256 + h * 128, 128), 128)
            picks_x[:, lanes] = jnp.where(rows == kx, 1.0, 0.0).astype(BF16)
            picks_y[:, lanes] = jnp.where(rows == ky, 1.0, 0.0).astype(BF16)

    recv_b[pl.ds(me, 1)] = send_b[pl.ds(me, 1)]
    cols_b[1]()
    for x in range(XN):
        for b in range(BN):
            piece = recv_b[8 * x + b].astype(F32)
            row = (x % 2) * 128 + (x // 2) * 64 + b * 4
            turn[row : row + 4, :] = piece[0:4]
            turn[row + 32 : row + 36, :] = piece[4:8]
    for x_lo in range(2):
        turned = turn[128 * x_lo : 128 * x_lo + 128, :].T
        for zi in range(3):
            stage[pl.ds(x_lo * 3 + zi, 16, stride=8), :] = turned[16 * zi : 16 * zi + 16]
    send_z[...] = stage[...].reshape(16, 8, 128).astype(BF16)
    cols_z[0]()
    proj_b[0]()
    recv_z[pl.ds(zz, 1)] = send_z[pl.ds(zz, 1)]

    atom_in.wait()
    coup_in.wait()
    atoms = lax.broadcasted_iota(jnp.int32, (64, 128), 0)
    marks = jnp.concatenate(
        [jnp.where(atoms == atom_ref[q : q + 1, :], 1.0, 0.0).astype(F32) for q in range(4)], axis=1
    )
    same = dot(marks.T.astype(BF16), marks.astype(BF16))
    coupled = jnp.where(same > 0.5, coup_ref[...], 0.0)
    part_h, part_l = split(coupled)
    coupled_h[...] = part_h
    coupled_l[...] = part_l

    lane8 = lax.broadcasted_iota(jnp.int32, (8, 128), 1)
    even = (lane8 // 32) % 2 == 0

    def scatter(t):
        for h, s in enumerate(sources(t)):
            first = recv_z[s].astype(F32)
            second = pltpu.roll(first, 5, 0)
            real = jnp.where(even, first, pltpu.roll(second, 32, 1))
            imag = jnp.where(even, pltpu.roll(first, 96, 1), second)
            spots = picks_x[:, pl.ds(pl.multiple_of(t * 256 + h * 128, 128), 128)]
            for i in range(6):
                value = (real, imag)[i % 2][i // 2 : i // 2 + 1]
                spread = jnp.broadcast_to(value, (GRID, 128)).astype(BF16)
                weights[i * 192 : (i + 1) * 192, h * 128 : (h + 1) * 128] = spots * spread
        grid_sum[...] += dot_nt(weights[...], picks_y[:, pl.ds(pl.multiple_of(t * 256, 256), 256)])

    cols_z[2](15).wait()
    scatter(0)

    rows8(recv_pb, me)[...] = rows8(send_pb, me)[...]
    proj_b[1]()
    total = recv_pb[0:8, :]
    for p in range(1, peers):
        total += recv_pb[8 * p : 8 * p + 8, :]
    send_pz[...] = total
    rows8(recv_pz, zz)[...] = total
    proj_z[0]()

    @pl.loop(1, 8)
    def _(t):
        cols_z[2](t).wait()
        cols_z[2](15 - t).wait()
        scatter(t)

    plane_in.wait()
    pot_in.wait()
    table = plane_ref[...]
    cos_h, sin_h, cos_l, sin_l = (table[192 * i : 192 * (i + 1)] for i in range(4))
    scale = 1.0 / float(GRID**3)

    def along_x(value):
        high, low = split(value)
        one = dot(table, high)
        two = dot(table[0:384], low)
        both = one[0:384] + one[384:768] + two
        return both[0:192], both[192:384]

    def one_plane(zi):
        rows = pl.ds(pl.multiple_of(zi * 384, 384), 384)
        start = grid_sum[rows, :].astype(BF16)
        by_cos = dot(start, cos_h) + dot(start, cos_l)
        by_sin = dot(start, sin_h) + dot(start, sin_l)
        real_c, real_s = along_x(by_cos[0:192] - by_sin[192:384])
        imag_c, imag_s = along_x(by_sin[0:192] + by_cos[192:384])
        field = pot_ref[zi] * scale
        real_c, real_s, imag_c, imag_s = along_x((real_c - imag_s) * field) + along_x((real_s + imag_c) * field)
        high, low = split(jnp.concatenate([real_c + imag_s, imag_c - real_s], axis=0))
        by_cos = dot(high, cos_h) + dot(high, cos_l) + dot(low, cos_h)
        by_sin = dot(high, sin_h) + dot(high, sin_l) + dot(low, sin_h)
        grid_back[rows, :] = jnp.concatenate(
            [by_cos[0:192] + by_sin[192:384], by_cos[192:384] - by_sin[0:192]], axis=0
        ).astype(BF16)

    @pl.loop(0, 2)
    def _(zi):
        one_plane(zi)

    proj_z[1]()
    total = recv_pz[0:8, :]
    for z in range(1, ZN):
        total += recv_pz[8 * z : 8 * z + 8, :]
    back_pb[...] = total
    rows8(got_pb, me)[...] = total
    sums_b[0]()
    one_plane(2)

    row8 = lax.broadcasted_iota(jnp.int32, (8, 128), 0)

    def gather(t):
        lanes = pl.ds(pl.multiple_of(t * 256, 256), 256)
        picked = dot(grid_back[...], picks_y[:, lanes])
        spots = picks_x[:, lanes].astype(F32)
        for i in range(6):
            value = jnp.sum(picked[i * 192 : (i + 1) * 192] * spots, axis=0, keepdims=True)
            for h in range(2):
                found[h * 16 + (i % 2) * 8 + i // 2 : h * 16 + (i % 2) * 8 + i // 2 + 1, :] = value[
                    :, h * 128 : (h + 1) * 128
                ]
        for h, s in enumerate(sources(t)):
            real = found[h * 16 : h * 16 + 8, :]
            imag = found[h * 16 + 8 : h * 16 + 16, :]
            upper = jnp.where(even, real, pltpu.roll(imag, 32, 1))
            lower = jnp.where(even, pltpu.roll(real, 96, 1), imag)
            back_z[s] = jnp.where(row8 < 3, upper, pltpu.roll(lower, 3, 0)).astype(BF16)

    @pl.loop(0, 7)
    def _(i):
        t = 7 - i
        gather(t)
        home_z[2](t + 1).start()
        home_z[2](16 - t).start()

    gather(0)
    home_z[2](1).start()
    got_z[pl.ds(zz, 1)] = back_z[pl.ds(zz, 1)]

    sums_b[1]()
    for part in range(4):
        real = got_pb[pl.ds(64 * part, 8, stride=8), :]
        imag = got_pb[pl.ds(64 * part + 1, 8, stride=8), :]
        pairs[part, pl.ds(0, 8, stride=2), :] = real
        pairs[part, pl.ds(1, 8, stride=2), :] = imag
        pairs[part, pl.ds(16, 8, stride=2), :] = -imag
        pairs[part, pl.ds(17, 8, stride=2), :] = real
    high, low = split(jnp.concatenate([pairs[part] for part in range(4)], axis=1))
    weighted = dot_nt(high, coupled_h[...]) + dot_nt(high, coupled_l[...]) + dot_nt(low, coupled_h[...])
    weighted = weighted.astype(BF16)
    for slot in range(4):
        mixed = dot_nt(weighted[0:16], proj_ref[slot * 192 : (slot + 1) * 192, :]) + dot_nt(
            weighted[16:32], proj_ref[(slot + 4) * 192 : (slot + 5) * 192, :]
        )
        wide[0, pl.ds(slot, 16, stride=4), :] = mixed[:, 0:128]
        wide[1, pl.ds(slot, 16, stride=4), :] = jnp.concatenate([mixed[:, 128:192], jnp.zeros((16, 64), F32)], axis=1)

    home_z[1]()
    stage[...] = got_z[...].astype(F32).reshape(128, 128)
    for x_lo in range(2):
        planes = [stage[pl.ds(x_lo * 3 + zi, 16, stride=8), :] for zi in range(3)]
        turned = jnp.concatenate(planes + [jnp.zeros((80, 128), F32)], axis=0).T
        for x_hi in range(2):
            for b in range(BN):
                row = x_hi * 64 + b * 4
                piece = jnp.concatenate([turned[row : row + 4], turned[row + 32 : row + 36]], axis=0)
                back_b[(x_hi * 2 + x_lo) * 8 + b] = piece.astype(BF16)
    home_b[0]()
    got_b[pl.ds(me, 1)] = back_b[pl.ds(me, 1)]
    home_b[1]()
    wave = jnp.concatenate([got_b[8 * x : 8 * x + 8].astype(F32).reshape(64, 128) for x in range(XN)], axis=1)
    part8 = (lax.broadcasted_iota(jnp.int32, (64, 512), 0) // 4) % 2
    turned = jnp.where(part8 == 0, pltpu.roll(wave, 60, 0), -pltpu.roll(wave, 4, 0)).astype(BF16)
    wave = wave.astype(BF16)
    local = (
        dot_nt(wave, ztab_ref[0:192, :])
        + dot_nt(wave, ztab_ref[384:576, :])
        + dot_nt(turned, ztab_ref[192:384, :])
        + dot_nt(turned, ztab_ref[576:768, :])
    )
    projected = jnp.concatenate([wide[0, 0:64, :], wide[1, 0:64, :]], axis=1)[:, 0:GRID]
    result = (local + projected) * active
    for i in range(16):
        out_ref[i] = result[4 * i : 4 * i + 4, :]


def on_device(orbitals, projectors, potential, couplings, atom_index, column_site, column_count):
    plane, ztab = (jnp.asarray(t) for t in make_tables())
    vmem = pl.BlockSpec(memory_space=pltpu.VMEM)
    hbm = pl.BlockSpec(memory_space=pltpu.HBM)
    smem = pl.BlockSpec(memory_space=pltpu.SMEM)
    flat = projectors.transpose(1, 2, 3, 0).reshape(8 * GRID, 512)
    scratch = lambda *shape: pltpu.VMEM(shape, F32)
    out = pl.pallas_call(
        kernel,
        out_shape=jax.ShapeDtypeStruct((16, 4, GRID), F32),
        in_specs=[smem] + [hbm] * 8,
        out_specs=vmem,
        scratch_shapes=[
            pltpu.VMEM((16, 128), jnp.int32),
            pltpu.VMEM((4, 128), jnp.int32),
            pltpu.VMEM((16, 4, GRID), BF16),
            pltpu.VMEM((8 * GRID, 512), BF16),
            scratch(3, GRID, GRID),
            scratch(512, 512),
            pltpu.VMEM((768, GRID), BF16),
            pltpu.VMEM((768, 512), BF16),
            scratch(64, GRID),
            scratch(64, GRID),
            scratch(2, 128, 128),
            pltpu.VMEM((32, 8, 128), BF16),
            pltpu.VMEM((32, 8, 128), BF16),
            scratch(256, 128),
            scratch(256, 128),
            scratch(256, 128),
            scratch(128, 128),
            pltpu.VMEM((16, 8, 128), BF16),
            pltpu.VMEM((16, 8, 128), BF16),
            scratch(8, 128),
            scratch(128, 128),
            pltpu.VMEM((GRID, 2048), BF16),
            pltpu.VMEM((GRID, 2048), BF16),
            pltpu.VMEM((1152, 256), BF16),
            scratch(1152, GRID),
            pltpu.VMEM((1152, GRID), BF16),
            pltpu.VMEM((512, 512), BF16),
            pltpu.VMEM((512, 512), BF16),
            scratch(32, 128),
            pltpu.VMEM((16, 8, 128), BF16),
            pltpu.VMEM((16, 8, 128), BF16),
            pltpu.VMEM((32, 8, 128), BF16),
            pltpu.VMEM((32, 8, 128), BF16),
            scratch(8, 128),
            scratch(256, 128),
            scratch(4, 32, 128),
            pltpu.SemaphoreType.DMA((2, 176)),
            pltpu.SemaphoreType.DMA((8,)),
        ],
        compiler_params=pltpu.CompilerParams(
            collective_id=0, has_side_effects=True, vmem_limit_bytes=67043328
        ),
    )(
        column_count,
        column_site.reshape(16, 128),
        atom_index.reshape(4, 128),
        orbitals.reshape(16, 4, GRID),
        flat,
        potential,
        couplings,
        plane,
        ztab,
    )
    return out.reshape(8, 2, 4, GRID)


def solution(mesh):
    return jax.shard_map(
        on_device,
        mesh=mesh,
        in_specs=(
            P(None, None, ("ga", "band"), None),
            P(None, None, ("ga", "band"), None),
            P("ga", None, None),
            P(),
            P(),
            P(),
            P(),
        ),
        out_specs=P(None, None, ("ga", "band"), None),
        check_vma=False,
    )
```

time: 75.4 us -> 60.6 us (0.80)
  local copies, waits for them, and re-layouts: 9.11 us -> 1.47 us
  Pallas kernels: 65.8 us -> 59 us
    unnamed x19 -> x1, local copies, waits for them, and re-layouts: 9.11 us -> 1.47 us
    pallas_call x1, Pallas kernels: 65.8 us -> 59 us  [on_device(): pl.pallas_call(kernel, out_shape=jax.ShapeDtypeStruct((16, 4, GRID), F32)...]
where the time goes in v1:
time: 60.6 us; the launch traced here: 60.5 us
  Pallas kernels  59 us (97%)
  local copies, waits for them, and re-layouts  1.47 us (2%)
    pallas_call x1, Pallas kernels, on_device(): pl.pallas_call(kernel, out_shape=jax.ShapeDtypeStruct((16, 4, GRID), F32)...  59 us
    unnamed x1, local copies, waits for them, and re-layouts  1.47 us

profile of v1, /device:TPU:1, one launch (start us, length us, event | category | flops | bytes accessed | tf_op | source)
XLA Modules:
  0.0 60.5 jit_solution(2004376977272514704)
XLA Ops:
  0.0 59.0 %shard_map.91 = f32[16,4,192]{2,1,0:T(4,128)} custom-call(s32[64]{0:T(128)} %count_ref.1, s32[16,128]{1,0:T(8,128)} %bitcast.10, s32[4,128]{1,0:T(4,128)} %bitcast.11, bf16[16,4,192]{2,1,0:T(4,128)(2,1)} %bitcast.9, bf16[1536,512]{1,0:T(8,128)(2,1)} %bitcast.7, f32[3,192,192]{2,1,0:T(8,128)} %pot_hbm.1, f32[512,512]{1,0:T(8,128)} %coup_hbm.1, ...), custom_call_target="tpu_custom_call" | custom-call | tf_op jit(solution)/shard_map/pallas_call | solution.py:393
  59.0 1.5 %copy.11 = f32[8,2,4,192]{3,2,1,0:T(4,128)} copy(f32[8,2,4,192]{3,2,1,0:T(4,128)} %bitcast.8) | data formatting | bytes 98304

commit v2 on v1

--- a/solution.py
+++ b/solution.py
@@ -80,41 +80,69 @@
         index = lax.rem(zz + d, ZN)
         return (index * XN + xx, band), index
 
-    def exchange(first_sem, size, where, source, target):
-        def copy(d):
-            device, index = where(d)
-            return pltpu.make_async_remote_copy(
-                src_ref=source(index),
-                dst_ref=target,
-                send_sem=sems.at[0, first_sem + d],
-                recv_sem=sems.at[1, first_sem + d],
-                device_id=device,
-                device_id_type=MESH,
-            )
-
-        def start():
-            @pl.loop(1, size)
-            def _(d):
-                copy(d).start()
-
-        def wait():
-            @pl.loop(1, size)
-            def _(d):
-                copy(d).wait()
-
-        return start, wait, copy
-
     def rows8(ref, index):
         return ref.at[pl.ds(pl.multiple_of(index * 8, 8), 8)]
 
     peers = XN * BN
-    cols_b = exchange(0, peers, on_plane, lambda i: send_b.at[i], recv_b.at[me])
-    proj_b = exchange(32, peers, on_plane, lambda i: rows8(send_pb, i), rows8(recv_pb, me))
-    cols_z = exchange(64, ZN, on_z, lambda i: send_z.at[i], recv_z.at[zz])
-    proj_z = exchange(80, ZN, on_z, lambda i: send_pz, rows8(recv_pz, zz))
-    sums_b = exchange(96, peers, on_plane, lambda i: back_pb, rows8(got_pb, me))
-    home_z = exchange(128, ZN, on_z, lambda i: back_z.at[i], got_z.at[zz])
-    home_b = exchange(144, peers, on_plane, lambda i: back_b.at[i], got_b.at[me])
+
+    def copy(number, target_of, source, target, arrival=None):
+        device, index = target_of
+        return pltpu.make_async_remote_copy(
+            src_ref=source(index),
+            dst_ref=target,
+            send_sem=sems.at[2 * number],
+            recv_sem=sems.at[2 * number + 1 if arrival is None else arrival],
+            device_id=device,
+            device_id_type=MESH,
+        )
+
+    def exchange(number, size, where, source, target, slots):
+        def start_one(d):
+            copy(number, where(d), source, target).start()
+
+        def start():
+            @pl.loop(0, size)
+            def _(i):
+                d = lax.rem(i + (20 if size == peers else 8), size)
+
+                @pl.when(d != 0)
+                def _():
+                    start_one(d)
+
+        def wait():
+            every = copy(number, (where(1)[0], 0), lambda i: slots, slots)
+            every.wait_send()
+            every.wait_recv()
+
+        return start, wait, start_one
+
+    cols_b = exchange(0, peers, on_plane, lambda i: send_b.at[i], recv_b.at[me], recv_b.at[pl.ds(0, peers - 1)])
+    proj_b = exchange(
+        1, peers, on_plane, lambda i: rows8(send_pb, i), rows8(recv_pb, me), recv_pb.at[pl.ds(0, 8 * peers - 8)]
+    )
+    proj_z = exchange(2, ZN, on_z, lambda i: send_pz, rows8(recv_pz, zz), recv_pz.at[pl.ds(0, 8 * ZN - 8)])
+    sums_b = exchange(3, peers, on_plane, lambda i: back_pb, rows8(got_pb, me), got_pb.at[pl.ds(0, 8 * peers - 8)])
+    home_z = exchange(4, ZN, on_z, lambda i: back_z.at[i], got_z.at[zz], got_z.at[pl.ds(0, ZN - 1)])
+    home_b = exchange(5, peers, on_plane, lambda i: back_b.at[i], got_b.at[me], got_b.at[pl.ds(0, peers - 1)])
+
+    def cols_z_start():
+        def one(d, pair):
+            copy(6, on_z(d), lambda i: send_z.at[i], recv_z.at[zz], 14 + pair).start()
+
+        @pl.loop(0, 7)
+        def _(i):
+            one(8 + i, 7 - i)
+            one(7 - i, 7 - i)
+
+        one(15, 0)
+
+    def cols_z_wait(pair, count):
+        slots = recv_z.at[pl.ds(0, count)]
+        copy(6, (on_z(1)[0], 0), lambda i: slots, slots, 14 + pair).wait_recv()
+
+    def cols_z_sent():
+        slots = recv_z.at[pl.ds(0, ZN - 1)]
+        copy(6, (on_z(1)[0], 0), lambda i: slots, slots, 14).wait_send()
 
     barrier = pltpu.get_barrier_semaphore()
     orb_in.start()
@@ -122,7 +150,7 @@
 
     @pl.loop(0, ZN - 1)
     def _(i):
-        away = lax.rem(i + 8, ZN - 1) + 1
+        away = lax.rem(i + 7, ZN - 1) + 1
         pl.semaphore_signal(barrier, inc=1, device_id=on_z(away)[0], device_id_type=MESH)
 
     @pl.loop(1, peers)
@@ -214,7 +242,7 @@
         for zi in range(3):
             stage[pl.ds(x_lo * 3 + zi, 16, stride=8), :] = turned[16 * zi : 16 * zi + 16]
     send_z[...] = stage[...].reshape(16, 8, 128).astype(BF16)
-    cols_z[0]()
+    cols_z_start()
     proj_b[0]()
     recv_z[pl.ds(zz, 1)] = send_z[pl.ds(zz, 1)]
 
@@ -246,7 +274,7 @@
                 weights[i * 192 : (i + 1) * 192, h * 128 : (h + 1) * 128] = spots * spread
         grid_sum[...] += dot_nt(weights[...], picks_y[:, pl.ds(pl.multiple_of(t * 256, 256), 256)])
 
-    cols_z[2](15).wait()
+    cols_z_wait(0, 1)
     scatter(0)
 
     rows8(recv_pb, me)[...] = rows8(send_pb, me)[...]
@@ -260,9 +288,10 @@
 
     @pl.loop(1, 8)
     def _(t):
-        cols_z[2](t).wait()
-        cols_z[2](15 - t).wait()
+        cols_z_wait(t, 2)
         scatter(t)
+
+    cols_z_sent()
 
     plane_in.wait()
     pot_in.wait()
@@ -329,11 +358,11 @@
     def _(i):
         t = 7 - i
         gather(t)
-        home_z[2](t + 1).start()
-        home_z[2](16 - t).start()
+        home_z[2](t + 1)
+        home_z[2](16 - t)
 
     gather(0)
-    home_z[2](1).start()
+    home_z[2](1)
     got_z[pl.ds(zz, 1)] = back_z[pl.ds(zz, 1)]
 
     sums_b[1]()
@@ -432,7 +461,7 @@
             scratch(8, 128),
             scratch(256, 128),
             scratch(4, 32, 128),
-            pltpu.SemaphoreType.DMA((2, 176)),
+            pltpu.SemaphoreType.DMA((22,)),
             pltpu.SemaphoreType.DMA((8,)),
         ],
         compiler_params=pltpu.CompilerParams(

time: 60.6 us -> 55.9 us (0.922)
  Pallas kernels: 59 us -> 54.2 us
    pallas_call x1, Pallas kernels: 59 us -> 54.2 us  [on_device(): pl.pallas_call(kernel, out_shape=jax.ShapeDtypeStruct((16, 4, GRID), F32)...]
where the time goes in v2:
time: 55.9 us; the launch traced here: 55.7 us
  Pallas kernels  54.2 us (97%)
  local copies, waits for them, and re-layouts  1.47 us (3%)
    pallas_call x1, Pallas kernels, on_device(): pl.pallas_call(kernel, out_shape=jax.ShapeDtypeStruct((16, 4, GRID), F32)...  54.2 us
    unnamed x1, local copies, waits for them, and re-layouts  1.47 us

profile of v2, /device:TPU:1, one launch (start us, length us, event | category | flops | bytes accessed | tf_op | source)
XLA Modules:
  0.0 55.7 jit_solution(934537657093465595)
XLA Ops:
  0.0 54.2 %shard_map.91 = f32[16,4,192]{2,1,0:T(4,128)} custom-call(s32[64]{0:T(128)} %count_ref.1, s32[16,128]{1,0:T(8,128)} %bitcast.10, s32[4,128]{1,0:T(4,128)} %bitcast.11, bf16[16,4,192]{2,1,0:T(4,128)(2,1)} %bitcast.9, bf16[1536,512]{1,0:T(8,128)(2,1)} %bitcast.7, f32[3,192,192]{2,1,0:T(8,128)} %pot_hbm.1, f32[512,512]{1,0:T(8,128)} %coup_hbm.1, ...), custom_call_target="tpu_custom_call" | custom-call | tf_op jit(solution)/shard_map/pallas_call | solution.py:422
  54.2 1.5 %copy.11 = f32[8,2,4,192]{3,2,1,0:T(4,128)} copy(f32[8,2,4,192]{3,2,1,0:T(4,128)} %bitcast.8) | data formatting | bytes 98304

commit v3 on v2

--- a/solution.py
+++ b/solution.py
@@ -25,18 +25,21 @@
 def make_tables():
     points = np.arange(GRID)
     phases = (points[:, None] * points[None, :] % GRID) * (2.0 * math.pi / GRID)
-    lanes = np.full((XN, 128), -1)
+    down = np.concatenate([np.cos(phases[0:97]), np.sin(phases[1:96])], axis=0)
+    plane = np.concatenate(split_host(np.ascontiguousarray(down.T)) + split_host(down), axis=0)
+    from_real = np.zeros((GRID, XN, 2, 64))
+    from_imag = np.zeros((GRID, XN, 2, 64))
     for x in range(XN):
         for sub in range(3):
-            lanes[x, 16 * sub : 16 * sub + 16] = 12 * np.arange(ZN) + 3 * x + sub
-    lanes = lanes.reshape(-1)
-    out = []
-    for pick in (points, lanes):
-        angles = phases[:, pick]
-        cos_h, cos_l = split_host(np.where(pick < 0, 0.0, np.cos(angles)))
-        sin_h, sin_l = split_host(np.where(pick < 0, 0.0, np.sin(angles)))
-        out.append(np.concatenate([cos_h, sin_h, cos_l, sin_l], axis=0))
-    return out
+            angles = phases[:, 12 * np.arange(ZN) + 3 * x + sub]
+            lanes = slice(16 * sub, 16 * sub + 16)
+            from_real[:, x, 0, lanes] = np.cos(angles)
+            from_real[:, x, 1, lanes] = np.sin(angles)
+            from_imag[:, x, 0, lanes] = -np.sin(angles)
+            from_imag[:, x, 1, lanes] = np.cos(angles)
+    real_h, real_l = split_host(from_real.reshape(GRID, 512))
+    imag_h, imag_l = split_host(from_imag.reshape(GRID, 512))
+    return plane, np.concatenate([real_h, imag_h, real_l, imag_l], axis=0)
 
 
 def dot(left, right):
@@ -55,9 +58,9 @@
 def kernel(
     count_ref, site_hbm, atom_hbm, orb_hbm, proj_hbm, pot_hbm, coup_hbm, plane_hbm, ztab_hbm, out_ref,
     site_ref, atom_ref, orb_ref, proj_ref, pot_ref, coup_ref, plane_ref, ztab_ref,
-    coef, coef_rot, wide, send_b, recv_b, send_pb, recv_pb, turn, stage, send_z, recv_z, send_pz, recv_pz,
+    wide, send_b, recv_b, send_pb, recv_pb, turn, stage, send_z, recv_z, send_pz, recv_pz,
     picks_x, picks_y, weights, grid_sum, grid_back, coupled_h, coupled_l, found, back_z, got_z,
-    back_b, got_b, back_pb, got_pb, pairs, sems, load_sems,
+    back_b, got_b, back_pb, got_pb, sems, load_sems,
 ):
     block = lax.axis_index("ga")
     band = lax.axis_index("band")
@@ -161,47 +164,45 @@
         load.start()
 
     used = count_ref[block]
-    row64 = lax.broadcasted_iota(jnp.int32, (64, GRID), 0)
-    active = jnp.where(band * 4 + row64 % 4 < used, 1.0, 0.0).astype(F32)
+    row32 = lax.broadcasted_iota(jnp.int32, (32, GRID), 0)
+    active = jnp.where(band * 4 + row32 % 4 < used, 1.0, 0.0).astype(F32)
     orb_in.wait()
     for n in range(8):
-        real = orb_ref[2 * n].astype(F32)
-        imag = orb_ref[2 * n + 1].astype(F32)
-        coef[8 * n : 8 * n + 4, :] = real
-        coef[8 * n + 4 : 8 * n + 8, :] = imag
-        coef_rot[8 * n : 8 * n + 4, :] = -imag
-        coef_rot[8 * n + 4 : 8 * n + 8, :] = real
-    coef[...] = coef[...] * active
-    coef_rot[...] = coef_rot[...] * active
-    plain = coef[...].astype(BF16)
-    rotated = coef_rot[...].astype(BF16)
+        for c in range(2):
+            piece = orb_ref[2 * n + c].astype(F32)
+            wide[0, 32 * c + 4 * n : 32 * c + 4 * n + 4, :] = piece[:, 0:128]
+            wide[1, 32 * c + 4 * n : 32 * c + 4 * n + 4, 0:64] = piece[:, 128:192]
+
+    def wide_rows(rows):
+        return jnp.concatenate([wide[h, rows, :] for h in range(2)], axis=1)[:, 0:GRID]
+
+    real = wide_rows(slice(0, 32)) * active
+    imag = wide_rows(slice(32, 64)) * active
+    for start, part in ((0, real), (32, imag), (64, -real)):
+        wide[0, start : start + 32, :] = part[:, 0:128]
+        wide[1, start : start + 32, 0:64] = part[:, 128:192]
+    real = real.astype(BF16)
+    imag = imag.astype(BF16)
     ztab_in.wait()
     along_z = (
-        dot(plain, ztab_ref[0:192, :])
-        + dot(plain, ztab_ref[384:576, :])
-        + dot(rotated, ztab_ref[192:384, :])
-        + dot(rotated, ztab_ref[576:768, :])
+        dot(real, ztab_ref[0:192, :])
+        + dot(real, ztab_ref[384:576, :])
+        + dot(imag, ztab_ref[192:384, :])
+        + dot(imag, ztab_ref[576:768, :])
     )
     for x in range(XN):
-        send_b[8 * x : 8 * x + 8] = along_z[:, 128 * x : 128 * x + 128].reshape(8, 8, 128).astype(BF16)
-
-    wide[0, 0:64, :] = coef[:, 0:128]
-    wide[1, 0:64, 0:64] = coef[:, 128:192]
-    wide[0, 64:128, :] = -coef_rot[:, 0:128]
-    wide[1, 64:128, 0:64] = -coef_rot[:, 128:192]
-
-    def slot_rows(start):
-        parts = [
-            jnp.concatenate([wide[h, pl.ds(start + 4 * c, 8, stride=8), :] for h in range(2)], axis=1)
-            for c in range(2)
-        ]
-        return jnp.concatenate(parts, axis=0)[:, 0:GRID].astype(BF16)
+        for n in range(8):
+            send_b[8 * x + n] = along_z[4 * n : 4 * n + 4, 128 * x : 128 * x + 128].astype(BF16)
+
+    def slot_rows(slot, starts):
+        parts = [wide_rows(pl.ds(start + slot, 8, stride=4)) for start in starts]
+        return jnp.concatenate(parts, axis=0).astype(BF16)
 
     proj_in.wait()
     partial = jnp.zeros((16, 512), F32)
     for slot in range(4):
-        partial += dot(slot_rows(slot), proj_ref[slot * 192 : (slot + 1) * 192, :])
-        partial += dot(slot_rows(64 + slot), proj_ref[(slot + 4) * 192 : (slot + 5) * 192, :])
+        partial += dot(slot_rows(slot, (0, 32)), proj_ref[slot * 192 : (slot + 1) * 192, :])
+        partial += dot(slot_rows(slot, (32, 64)), proj_ref[(slot + 4) * 192 : (slot + 5) * 192, :])
     send_pb[...] = jnp.zeros_like(send_pb)
     for x in range(XN):
         for c in range(2):
@@ -218,29 +219,32 @@
     def sources(t):
         return lax.rem(zz + ZN - t, ZN), lax.rem(zz + t + 1, ZN)
 
+    rows = lax.broadcasted_iota(jnp.int32, (GRID, 128), 0)
+    is_even = rows < 97
+    frequency = jnp.where(is_even, rows, rows - 96)
+
+    def folded(position):
+        distance = jnp.minimum(position, GRID - position)
+        sign = jnp.where(position < 96, 1.0, -1.0).astype(F32)
+        return jnp.where(frequency == distance, jnp.where(is_even, 1.0, sign), 0.0).astype(BF16)
+
     @pl.loop(0, 8)
     def _(t):
-        rows = lax.broadcasted_iota(jnp.int32, (GRID, 128), 0)
         for h, s in enumerate(sources(t)):
             site = site_ref[pl.ds(s, 1), :]
             kx = (site * 43691) >> 23
-            ky = site - kx * 192
             lanes = pl.ds(pl.multiple_of(t * 256 + h * 128, 128), 128)
-            picks_x[:, lanes] = jnp.where(rows == kx, 1.0, 0.0).astype(BF16)
-            picks_y[:, lanes] = jnp.where(rows == ky, 1.0, 0.0).astype(BF16)
+            picks_x[:, lanes] = folded(kx)
+            picks_y[:, lanes] = folded(site - kx * 192)
 
     recv_b[pl.ds(me, 1)] = send_b[pl.ds(me, 1)]
     cols_b[1]()
-    for x in range(XN):
-        for b in range(BN):
-            piece = recv_b[8 * x + b].astype(F32)
-            row = (x % 2) * 128 + (x // 2) * 64 + b * 4
-            turn[row : row + 4, :] = piece[0:4]
-            turn[row + 32 : row + 36, :] = piece[4:8]
-    for x_lo in range(2):
-        turned = turn[128 * x_lo : 128 * x_lo + 128, :].T
+    for p in range(peers):
+        turn[4 * p : 4 * p + 4, :] = recv_b[p].astype(F32)
+    turned = turn[...].T
+    for c in range(2):
         for zi in range(3):
-            stage[pl.ds(x_lo * 3 + zi, 16, stride=8), :] = turned[16 * zi : 16 * zi + 16]
+            stage[pl.ds(c * 3 + zi, 16, stride=8), :] = turned[64 * c + 16 * zi : 64 * c + 16 * zi + 16]
     send_z[...] = stage[...].reshape(16, 8, 128).astype(BF16)
     cols_z_start()
     proj_b[0]()
@@ -258,18 +262,13 @@
     coupled_h[...] = part_h
     coupled_l[...] = part_l
 
-    lane8 = lax.broadcasted_iota(jnp.int32, (8, 128), 1)
-    even = (lane8 // 32) % 2 == 0
-
     def scatter(t):
         for h, s in enumerate(sources(t)):
-            first = recv_z[s].astype(F32)
-            second = pltpu.roll(first, 5, 0)
-            real = jnp.where(even, first, pltpu.roll(second, 32, 1))
-            imag = jnp.where(even, pltpu.roll(first, 96, 1), second)
+            arrived = recv_z[s].astype(F32)
             spots = picks_x[:, pl.ds(pl.multiple_of(t * 256 + h * 128, 128), 128)]
             for i in range(6):
-                value = (real, imag)[i % 2][i // 2 : i // 2 + 1]
+                row = (i % 2) * 3 + i // 2
+                value = arrived[row : row + 1]
                 spread = jnp.broadcast_to(value, (GRID, 128)).astype(BF16)
                 weights[i * 192 : (i + 1) * 192, h * 128 : (h + 1) * 128] = spots * spread
         grid_sum[...] += dot_nt(weights[...], picks_y[:, pl.ds(pl.multiple_of(t * 256, 256), 256)])
@@ -295,32 +294,45 @@
 
     plane_in.wait()
     pot_in.wait()
-    table = plane_ref[...]
-    cos_h, sin_h, cos_l, sin_l = (table[192 * i : 192 * (i + 1)] for i in range(4))
+    across_h = plane_ref[0:192, :]
+    across_l = plane_ref[192:384, :]
+    down_h = plane_ref[384:576, :]
+    down_l = plane_ref[576:768, :]
     scale = 1.0 / float(GRID**3)
-
-    def along_x(value):
+    even_row = lax.broadcasted_iota(jnp.int32, (GRID, GRID), 0) < 97
+    even_lane = lax.broadcasted_iota(jnp.int32, (GRID, GRID), 1) < 97
+
+    def times_i(even, real, imag):
+        return jnp.where(even, real, -imag), jnp.where(even, imag, real)
+
+    def times_minus_i(even, real, imag):
+        return jnp.where(even, real, imag), jnp.where(even, imag, -real)
+
+    def from_left(first, value):
         high, low = split(value)
-        one = dot(table, high)
-        two = dot(table[0:384], low)
-        both = one[0:384] + one[384:768] + two
+        both = dot(plane_ref[first : first + 384, :], high)
+        return both[0:192] + both[192:384] + dot(plane_ref[first : first + 192, :], low)
+
+    def from_right(real, imag, table_h, table_l):
+        high, low = split(jnp.concatenate([real, imag], axis=0))
+        both = dot(high, table_h) + dot(high, table_l) + dot(low, table_h)
         return both[0:192], both[192:384]
 
     def one_plane(zi):
         rows = pl.ds(pl.multiple_of(zi * 384, 384), 384)
-        start = grid_sum[rows, :].astype(BF16)
-        by_cos = dot(start, cos_h) + dot(start, cos_l)
-        by_sin = dot(start, sin_h) + dot(start, sin_l)
-        real_c, real_s = along_x(by_cos[0:192] - by_sin[192:384])
-        imag_c, imag_s = along_x(by_sin[0:192] + by_cos[192:384])
+        start = grid_sum[rows, :]
+        real, imag = times_i(even_lane, start[0:192], start[192:384])
+        real, imag = from_right(real, imag, down_h, down_l)
+        real, imag = times_i(even_row, real, imag)
         field = pot_ref[zi] * scale
-        real_c, real_s, imag_c, imag_s = along_x((real_c - imag_s) * field) + along_x((real_s + imag_c) * field)
-        high, low = split(jnp.concatenate([real_c + imag_s, imag_c - real_s], axis=0))
-        by_cos = dot(high, cos_h) + dot(high, cos_l) + dot(low, cos_h)
-        by_sin = dot(high, sin_h) + dot(high, sin_l) + dot(low, sin_h)
-        grid_back[rows, :] = jnp.concatenate(
-            [by_cos[0:192] + by_sin[192:384], by_cos[192:384] - by_sin[0:192]], axis=0
-        ).astype(BF16)
+        real = from_left(0, real) * field
+        imag = from_left(0, imag) * field
+        real = from_left(384, real)
+        imag = from_left(384, imag)
+        real, imag = times_minus_i(even_row, real, imag)
+        real, imag = from_right(real, imag, across_h, across_l)
+        real, imag = times_minus_i(even_lane, real, imag)
+        grid_back[rows, :] = jnp.concatenate([real, imag], axis=0).astype(BF16)
 
     @pl.loop(0, 2)
     def _(zi):
@@ -335,8 +347,6 @@
     sums_b[0]()
     one_plane(2)
 
-    row8 = lax.broadcasted_iota(jnp.int32, (8, 128), 0)
-
     def gather(t):
         lanes = pl.ds(pl.multiple_of(t * 256, 256), 256)
         picked = dot(grid_back[...], picks_y[:, lanes])
@@ -344,15 +354,10 @@
         for i in range(6):
             value = jnp.sum(picked[i * 192 : (i + 1) * 192] * spots, axis=0, keepdims=True)
             for h in range(2):
-                found[h * 16 + (i % 2) * 8 + i // 2 : h * 16 + (i % 2) * 8 + i // 2 + 1, :] = value[
-                    :, h * 128 : (h + 1) * 128
-                ]
+                row = h * 8 + (i % 2) * 3 + i // 2
+                found[row : row + 1, :] = value[:, h * 128 : (h + 1) * 128]
         for h, s in enumerate(sources(t)):
-            real = found[h * 16 : h * 16 + 8, :]
-            imag = found[h * 16 + 8 : h * 16 + 16, :]
-            upper = jnp.where(even, real, pltpu.roll(imag, 32, 1))
-            lower = jnp.where(even, pltpu.roll(real, 96, 1), imag)
-            back_z[s] = jnp.where(row8 < 3, upper, pltpu.roll(lower, 3, 0)).astype(BF16)
+            back_z[s] = found[8 * h : 8 * h + 8, :]
 
     @pl.loop(0, 7)
     def _(i):
@@ -366,50 +371,46 @@
     got_z[pl.ds(zz, 1)] = back_z[pl.ds(zz, 1)]
 
     sums_b[1]()
+    pairs = []
     for part in range(4):
         real = got_pb[pl.ds(64 * part, 8, stride=8), :]
         imag = got_pb[pl.ds(64 * part + 1, 8, stride=8), :]
-        pairs[part, pl.ds(0, 8, stride=2), :] = real
-        pairs[part, pl.ds(1, 8, stride=2), :] = imag
-        pairs[part, pl.ds(16, 8, stride=2), :] = -imag
-        pairs[part, pl.ds(17, 8, stride=2), :] = real
-    high, low = split(jnp.concatenate([pairs[part] for part in range(4)], axis=1))
+        pairs.append(jnp.concatenate([real, imag, -imag, real], axis=0))
+    high, low = split(jnp.concatenate(pairs, axis=1))
     weighted = dot_nt(high, coupled_h[...]) + dot_nt(high, coupled_l[...]) + dot_nt(low, coupled_h[...])
     weighted = weighted.astype(BF16)
     for slot in range(4):
         mixed = dot_nt(weighted[0:16], proj_ref[slot * 192 : (slot + 1) * 192, :]) + dot_nt(
             weighted[16:32], proj_ref[(slot + 4) * 192 : (slot + 5) * 192, :]
         )
-        wide[0, pl.ds(slot, 16, stride=4), :] = mixed[:, 0:128]
-        wide[1, pl.ds(slot, 16, stride=4), :] = jnp.concatenate([mixed[:, 128:192], jnp.zeros((16, 64), F32)], axis=1)
+        mixed = jnp.concatenate([mixed, jnp.zeros((16, 64), F32)], axis=1)
+        for c in range(2):
+            for h in range(2):
+                wide[h, pl.ds(32 * c + slot, 8, stride=4), :] = mixed[8 * c : 8 * c + 8, 128 * h : 128 * h + 128]
 
     home_z[1]()
-    stage[...] = got_z[...].astype(F32).reshape(128, 128)
-    for x_lo in range(2):
-        planes = [stage[pl.ds(x_lo * 3 + zi, 16, stride=8), :] for zi in range(3)]
-        turned = jnp.concatenate(planes + [jnp.zeros((80, 128), F32)], axis=0).T
-        for x_hi in range(2):
-            for b in range(BN):
-                row = x_hi * 64 + b * 4
-                piece = jnp.concatenate([turned[row : row + 4], turned[row + 32 : row + 36]], axis=0)
-                back_b[(x_hi * 2 + x_lo) * 8 + b] = piece.astype(BF16)
+    stage[...] = got_z[...].reshape(128, 128)
+    rows = []
+    for c in range(2):
+        rows += [stage[pl.ds(c * 3 + zi, 16, stride=8), :] for zi in range(3)]
+        rows.append(jnp.zeros((16, 128), F32))
+    turned = jnp.concatenate(rows, axis=0).T
+    for p in range(peers):
+        back_b[p] = turned[4 * p : 4 * p + 4]
     home_b[0]()
     got_b[pl.ds(me, 1)] = back_b[pl.ds(me, 1)]
     home_b[1]()
-    wave = jnp.concatenate([got_b[8 * x : 8 * x + 8].astype(F32).reshape(64, 128) for x in range(XN)], axis=1)
-    part8 = (lax.broadcasted_iota(jnp.int32, (64, 512), 0) // 4) % 2
-    turned = jnp.where(part8 == 0, pltpu.roll(wave, 60, 0), -pltpu.roll(wave, 4, 0)).astype(BF16)
-    wave = wave.astype(BF16)
-    local = (
-        dot_nt(wave, ztab_ref[0:192, :])
-        + dot_nt(wave, ztab_ref[384:576, :])
-        + dot_nt(turned, ztab_ref[192:384, :])
-        + dot_nt(turned, ztab_ref[576:768, :])
-    )
-    projected = jnp.concatenate([wide[0, 0:64, :], wide[1, 0:64, :]], axis=1)[:, 0:GRID]
-    result = (local + projected) * active
-    for i in range(16):
-        out_ref[i] = result[4 * i : 4 * i + 4, :]
+    for x in range(XN):
+        for n in range(8):
+            turn[32 * x + 4 * n : 32 * x + 4 * n + 4, :] = got_b[8 * x + n]
+    wave = jnp.concatenate([turn[32 * x : 32 * x + 32, :] for x in range(XN)], axis=1)
+    high, low = split(wave)
+    for c in range(2):
+        table_h = ztab_ref[192 * c : 192 * c + 192, :]
+        local = dot_nt(high, table_h) + dot_nt(high, ztab_ref[192 * c + 384 : 192 * c + 576, :]) + dot_nt(low, table_h)
+        result = (local + wide_rows(slice(32 * c, 32 * c + 32))) * active
+        for n in range(8):
+            out_ref[2 * n + c] = result[4 * n : 4 * n + 4, :]
 
 
 def on_device(orbitals, projectors, potential, couplings, atom_index, column_site, column_count):
@@ -433,14 +434,12 @@
             scratch(512, 512),
             pltpu.VMEM((768, GRID), BF16),
             pltpu.VMEM((768, 512), BF16),
-            scratch(64, GRID),
-            scratch(64, GRID),
             scratch(2, 128, 128),
-            pltpu.VMEM((32, 8, 128), BF16),
-            pltpu.VMEM((32, 8, 128), BF16),
+            pltpu.VMEM((32, 4, 128), BF16),
+            pltpu.VMEM((32, 4, 128), BF16),
             scratch(256, 128),
             scratch(256, 128),
-            scratch(256, 128),
+            scratch(128, 128),
             scratch(128, 128),
             pltpu.VMEM((16, 8, 128), BF16),
             pltpu.VMEM((16, 8, 128), BF16),
@@ -453,14 +452,13 @@
             pltpu.VMEM((1152, GRID), BF16),
             pltpu.VMEM((512, 512), BF16),
             pltpu.VMEM((512, 512), BF16),
-            scratch(32, 128),
-            pltpu.VMEM((16, 8, 128), BF16),
-            pltpu.VMEM((16, 8, 128), BF16),
-            pltpu.VMEM((32, 8, 128), BF16),
-            pltpu.VMEM((32, 8, 128), BF16),
+            scratch(16, 128),
+            scratch(16, 8, 128),
+            scratch(16, 8, 128),
+            scratch(32, 4, 128),
+            scratch(32, 4, 128),
             scratch(8, 128),
             scratch(256, 128),
-            scratch(4, 32, 128),
             pltpu.SemaphoreType.DMA((22,)),
             pltpu.SemaphoreType.DMA((8,)),
         ],

time: 55.9 us -> 54.3 us (0.971)
  Pallas kernels: 54.2 us -> 52.6 us
    pallas_call x1, Pallas kernels: 54.2 us -> 52.6 us  [on_device(): pl.pallas_call(kernel, out_shape=jax.ShapeDtypeStruct((16, 4, GRID), F32)...]
where the time goes in v3:
time: 54.3 us; the launch traced here: 54.1 us
  Pallas kernels  52.6 us (97%)
  local copies, waits for them, and re-layouts  1.47 us (3%)
    pallas_call x1, Pallas kernels, on_device(): pl.pallas_call(kernel, out_shape=jax.ShapeDtypeStruct((16, 4, GRID), F32)...  52.6 us
    unnamed x1, local copies, waits for them, and re-layouts  1.47 us

profile of v3, /device:TPU:1, one launch (start us, length us, event | category | flops | bytes accessed | tf_op | source)
XLA Modules:
  0.0 54.1 jit_solution(13508011850864727607)
XLA Ops:
  0.0 52.6 %shard_map.91 = f32[16,4,192]{2,1,0:T(4,128)} custom-call(s32[64]{0:T(128)} %count_ref.1, s32[16,128]{1,0:T(8,128)} %bitcast.10, s32[4,128]{1,0:T(4,128)} %bitcast.11, bf16[16,4,192]{2,1,0:T(4,128)(2,1)} %bitcast.9, bf16[1536,512]{1,0:T(8,128)(2,1)} %bitcast.7, f32[3,192,192]{2,1,0:T(8,128)} %pot_hbm.1, f32[512,512]{1,0:T(8,128)} %coup_hbm.1, ...), custom_call_target="tpu_custom_call" | custom-call | tf_op jit(solution)/shard_map/pallas_call | solution.py:423
  52.7 1.5 %copy.11 = f32[8,2,4,192]{3,2,1,0:T(4,128)} copy(f32[8,2,4,192]{3,2,1,0:T(4,128)} %bitcast.8) | data formatting | bytes 98304

commit v4 on v3

--- a/solution.py
+++ b/solution.py
@@ -14,6 +14,10 @@
 BF16 = jnp.bfloat16
 GRID = 192
 ZN, XN, BN = 16, 4, 8
+FAR_FIRST = {
+    ZN: [8, 9, 7, 10, 6, 11, 5, 12, 4, 13, 3, 14, 2, 15, 1],
+    XN * BN: [d % 32 for d in range(20, 52) if d != 32],
+}
 
 
 def split_host(table):
@@ -83,9 +87,6 @@
         index = lax.rem(zz + d, ZN)
         return (index * XN + xx, band), index
 
-    def rows8(ref, index):
-        return ref.at[pl.ds(pl.multiple_of(index * 8, 8), 8)]
-
     peers = XN * BN
 
     def copy(number, target_of, source, target, arrival=None):
@@ -104,13 +105,8 @@
             copy(number, where(d), source, target).start()
 
         def start():
-            @pl.loop(0, size)
-            def _(i):
-                d = lax.rem(i + (20 if size == peers else 8), size)
-
-                @pl.when(d != 0)
-                def _():
-                    start_one(d)
+            for d in FAR_FIRST[size]:
+                start_one(d)
 
         def wait():
             every = copy(number, (where(1)[0], 0), lambda i: slots, slots)
@@ -120,11 +116,9 @@
         return start, wait, start_one
 
     cols_b = exchange(0, peers, on_plane, lambda i: send_b.at[i], recv_b.at[me], recv_b.at[pl.ds(0, peers - 1)])
-    proj_b = exchange(
-        1, peers, on_plane, lambda i: rows8(send_pb, i), rows8(recv_pb, me), recv_pb.at[pl.ds(0, 8 * peers - 8)]
-    )
-    proj_z = exchange(2, ZN, on_z, lambda i: send_pz, rows8(recv_pz, zz), recv_pz.at[pl.ds(0, 8 * ZN - 8)])
-    sums_b = exchange(3, peers, on_plane, lambda i: back_pb, rows8(got_pb, me), got_pb.at[pl.ds(0, 8 * peers - 8)])
+    proj_b = exchange(1, peers, on_plane, lambda i: send_pb.at[i], recv_pb.at[me], recv_pb.at[pl.ds(0, peers - 1)])
+    proj_z = exchange(2, ZN, on_z, lambda i: send_pz, recv_pz.at[zz], recv_pz.at[pl.ds(0, ZN - 1)])
+    sums_b = exchange(3, peers, on_plane, lambda i: back_pb, got_pb.at[me], got_pb.at[pl.ds(0, peers - 1)])
     home_z = exchange(4, ZN, on_z, lambda i: back_z.at[i], got_z.at[zz], got_z.at[pl.ds(0, ZN - 1)])
     home_b = exchange(5, peers, on_plane, lambda i: back_b.at[i], got_b.at[me], got_b.at[pl.ds(0, peers - 1)])
 
@@ -132,11 +126,9 @@
         def one(d, pair):
             copy(6, on_z(d), lambda i: send_z.at[i], recv_z.at[zz], 14 + pair).start()
 
-        @pl.loop(0, 7)
-        def _(i):
-            one(8 + i, 7 - i)
-            one(7 - i, 7 - i)
-
+        for pair in range(7, 0, -1):
+            one(15 - pair, pair)
+            one(pair, pair)
         one(15, 0)
 
     def cols_z_wait(pair, count):
@@ -151,13 +143,9 @@
     orb_in.start()
     ztab_in.start()
 
-    @pl.loop(0, ZN - 1)
-    def _(i):
-        away = lax.rem(i + 7, ZN - 1) + 1
-        pl.semaphore_signal(barrier, inc=1, device_id=on_z(away)[0], device_id_type=MESH)
-
-    @pl.loop(1, peers)
-    def _(d):
+    for d in FAR_FIRST[ZN]:
+        pl.semaphore_signal(barrier, inc=1, device_id=on_z(d)[0], device_id_type=MESH)
+    for d in FAR_FIRST[peers]:
         pl.semaphore_signal(barrier, inc=1, device_id=on_plane(d)[0], device_id_type=MESH)
 
     for load in loads[2:]:
@@ -203,13 +191,13 @@
     for slot in range(4):
         partial += dot(slot_rows(slot, (0, 32)), proj_ref[slot * 192 : (slot + 1) * 192, :])
         partial += dot(slot_rows(slot, (32, 64)), proj_ref[(slot + 4) * 192 : (slot + 5) * 192, :])
-    send_pb[...] = jnp.zeros_like(send_pb)
     for x in range(XN):
         for c in range(2):
-            send_pb[pl.ds(64 * x + c, 8, stride=8), :] = partial[8 * c : 8 * c + 8, 128 * x : 128 * x + 128]
+            send_pb[8 * x : 8 * x + 8, c, :] = partial[8 * c : 8 * c + 8, 128 * x : 128 * x + 128]
 
     pl.semaphore_wait(barrier, ZN + peers - 2)
     cols_b[0]()
+    proj_b[0]()
 
     stage[...] = jnp.zeros_like(stage)
     found[...] = jnp.zeros_like(found)
@@ -247,8 +235,16 @@
             stage[pl.ds(c * 3 + zi, 16, stride=8), :] = turned[64 * c + 16 * zi : 64 * c + 16 * zi + 16]
     send_z[...] = stage[...].reshape(16, 8, 128).astype(BF16)
     cols_z_start()
-    proj_b[0]()
     recv_z[pl.ds(zz, 1)] = send_z[pl.ds(zz, 1)]
+
+    recv_pb[pl.ds(me, 1)] = send_pb[pl.ds(me, 1)]
+    proj_b[1]()
+    total = recv_pb[0]
+    for p in range(1, peers):
+        total += recv_pb[p]
+    send_pz[...] = total
+    recv_pz[pl.ds(zz, 1)] = total[None]
+    proj_z[0]()
 
     atom_in.wait()
     coup_in.wait()
@@ -275,15 +271,6 @@
 
     cols_z_wait(0, 1)
     scatter(0)
-
-    rows8(recv_pb, me)[...] = rows8(send_pb, me)[...]
-    proj_b[1]()
-    total = recv_pb[0:8, :]
-    for p in range(1, peers):
-        total += recv_pb[8 * p : 8 * p + 8, :]
-    send_pz[...] = total
-    rows8(recv_pz, zz)[...] = total
-    proj_z[0]()
 
     @pl.loop(1, 8)
     def _(t):
@@ -334,18 +321,19 @@
         real, imag = times_minus_i(even_lane, real, imag)
         grid_back[rows, :] = jnp.concatenate([real, imag], axis=0).astype(BF16)
 
-    @pl.loop(0, 2)
+    one_plane(0)
+
+    proj_z[1]()
+    total = recv_pz[0]
+    for z in range(1, ZN):
+        total += recv_pz[z]
+    back_pb[...] = total
+    got_pb[pl.ds(me, 1)] = total[None]
+    sums_b[0]()
+
+    @pl.loop(1, 3)
     def _(zi):
         one_plane(zi)
-
-    proj_z[1]()
-    total = recv_pz[0:8, :]
-    for z in range(1, ZN):
-        total += recv_pz[8 * z : 8 * z + 8, :]
-    back_pb[...] = total
-    rows8(got_pb, me)[...] = total
-    sums_b[0]()
-    one_plane(2)
 
     def gather(t):
         lanes = pl.ds(pl.multiple_of(t * 256, 256), 256)
@@ -373,8 +361,8 @@
     sums_b[1]()
     pairs = []
     for part in range(4):
-        real = got_pb[pl.ds(64 * part, 8, stride=8), :]
-        imag = got_pb[pl.ds(64 * part + 1, 8, stride=8), :]
+        real = got_pb[8 * part : 8 * part + 8, 0, :]
+        imag = got_pb[8 * part : 8 * part + 8, 1, :]
         pairs.append(jnp.concatenate([real, imag, -imag, real], axis=0))
     high, low = split(jnp.concatenate(pairs, axis=1))
     weighted = dot_nt(high, coupled_h[...]) + dot_nt(high, coupled_l[...]) + dot_nt(low, coupled_h[...])
@@ -422,7 +410,7 @@
     scratch = lambda *shape: pltpu.VMEM(shape, F32)
     out = pl.pallas_call(
         kernel,
-        out_shape=jax.ShapeDtypeStruct((16, 4, GRID), F32),
+        out_shape=pltpu.VMEM((16, 4, GRID), F32),
         in_specs=[smem] + [hbm] * 8,
         out_specs=vmem,
         scratch_shapes=[
@@ -437,14 +425,14 @@
             scratch(2, 128, 128),
             pltpu.VMEM((32, 4, 128), BF16),
             pltpu.VMEM((32, 4, 128), BF16),
-            scratch(256, 128),
-            scratch(256, 128),
+            scratch(32, 2, 128),
+            scratch(32, 2, 128),
             scratch(128, 128),
             scratch(128, 128),
             pltpu.VMEM((16, 8, 128), BF16),
             pltpu.VMEM((16, 8, 128), BF16),
-            scratch(8, 128),
-            scratch(128, 128),
+            scratch(2, 128),
+            scratch(16, 2, 128),
             pltpu.VMEM((GRID, 2048), BF16),
             pltpu.VMEM((GRID, 2048), BF16),
             pltpu.VMEM((1152, 256), BF16),
@@ -457,13 +445,13 @@
             scratch(16, 8, 128),
             scratch(32, 4, 128),
             scratch(32, 4, 128),
-            scratch(8, 128),
-            scratch(256, 128),
+            scratch(2, 128),
+            scratch(32, 2, 128),
             pltpu.SemaphoreType.DMA((22,)),
             pltpu.SemaphoreType.DMA((8,)),
         ],
         compiler_params=pltpu.CompilerParams(
-            collective_id=0, has_side_effects=True, vmem_limit_bytes=67043328
+            collective_id=0, has_side_effects=True, vmem_limit_bytes=60000000
         ),
     )(
         column_count,

time: 54.3 us -> 48.3 us (0.89)
  Pallas kernels: 52.6 us -> 47.6 us
  local copies, waits for them, and re-layouts: 1.47 us -> 0.63 us
    pallas_call x1, Pallas kernels: 52.6 us -> 47.6 us  [on_device(): pl.pallas_call(kernel, out_shape=pltpu.VMEM((16, 4, GRID), F32), in_specs...]
    unnamed x1, local copies, waits for them, and re-layouts: 1.47 us -> 0.63 us
where the time goes in v4:
time: 48.3 us; the launch traced here: 48.2 us
  Pallas kernels  47.6 us (99%)
  local copies, waits for them, and re-layouts  0.63 us (1%)
    pallas_call x1, Pallas kernels, on_device(): pl.pallas_call(kernel, out_shape=pltpu.VMEM((16, 4, GRID), F32), in_specs...  47.6 us

profile of v4, /device:TPU:1, one launch (start us, length us, event | category | flops | bytes accessed | tf_op | source)
XLA Modules:
  0.0 48.2 jit_solution(3806184969396878694)
XLA Ops:
  0.0 47.6 %shard_map.91 = f32[16,4,192]{2,1,0:T(4,128)S(1)} custom-call(s32[64]{0:T(128)} %count_ref.1, s32[16,128]{1,0:T(8,128)} %bitcast.10, s32[4,128]{1,0:T(4,128)} %bitcast.11, bf16[16,4,192]{2,1,0:T(4,128)(2,1)} %bitcast.9, bf16[1536,512]{1,0:T(8,128)(2,1)} %bitcast.8, f32[3,192,192]{2,1,0:T(8,128)} %pot_hbm.1, f32[512,512]{1,0:T(8,128)} %coup_hbm.1, ...), custom_call_target="tpu_custom_call" | custom-call | tf_op jit(solution)/shard_map/pallas_call | solution.py:411
  47.6 0.6 %copy.11 = f32[8,2,4,192]{3,2,1,0:T(4,128)} copy(f32[8,2,4,192]{3,2,1,0:T(4,128)S(1)} %bitcast.7) | data formatting | bytes 98304

commit v5 on v4

--- a/solution.py
+++ b/solution.py
@@ -64,7 +64,7 @@
     site_ref, atom_ref, orb_ref, proj_ref, pot_ref, coup_ref, plane_ref, ztab_ref,
     wide, send_b, recv_b, send_pb, recv_pb, turn, stage, send_z, recv_z, send_pz, recv_pz,
     picks_x, picks_y, weights, grid_sum, grid_back, coupled_h, coupled_l, found, back_z, got_z,
-    back_b, got_b, back_pb, got_pb, sems, load_sems,
+    back_b, got_b, back_pb, got_pb, sems, load_sems, relays,
 ):
     block = lax.axis_index("ga")
     band = lax.axis_index("band")
@@ -143,10 +143,19 @@
     orb_in.start()
     ztab_in.start()
 
-    for d in FAR_FIRST[ZN]:
-        pl.semaphore_signal(barrier, inc=1, device_id=on_z(d)[0], device_id_type=MESH)
     for d in FAR_FIRST[peers]:
         pl.semaphore_signal(barrier, inc=1, device_id=on_plane(d)[0], device_id_type=MESH)
+    for d in (1, ZN - 1):
+        pl.semaphore_signal(barrier, inc=1, device_id=on_z(d)[0], device_id_type=MESH)
+
+    def relay(k):
+        for side, d in enumerate((1, ZN - 1)):
+            pl.semaphore_signal(relays.at[2 * k + side], inc=1, device_id=on_z(d)[0], device_id_type=MESH)
+
+    def relayed(k):
+        for side in range(2):
+            pl.semaphore_wait(relays.at[2 * k + side], 1)
+
 
     for load in loads[2:]:
         load.start()
@@ -182,6 +191,10 @@
         for n in range(8):
             send_b[8 * x + n] = along_z[4 * n : 4 * n + 4, 128 * x : 128 * x + 128].astype(BF16)
 
+    pl.semaphore_wait(barrier, peers + 1)
+    cols_b[0]()
+    relay(0)
+
     def slot_rows(slot, starts):
         parts = [wide_rows(pl.ds(start + slot, 8, stride=4)) for start in starts]
         return jnp.concatenate(parts, axis=0).astype(BF16)
@@ -194,10 +207,9 @@
     for x in range(XN):
         for c in range(2):
             send_pb[8 * x : 8 * x + 8, c, :] = partial[8 * c : 8 * c + 8, 128 * x : 128 * x + 128]
-
-    pl.semaphore_wait(barrier, ZN + peers - 2)
-    cols_b[0]()
     proj_b[0]()
+    relayed(0)
+    relay(1)
 
     stage[...] = jnp.zeros_like(stage)
     found[...] = jnp.zeros_like(found)
@@ -216,14 +228,23 @@
         sign = jnp.where(position < 96, 1.0, -1.0).astype(F32)
         return jnp.where(frequency == distance, jnp.where(is_even, 1.0, sign), 0.0).astype(BF16)
 
-    @pl.loop(0, 8)
-    def _(t):
+    def pick(t):
         for h, s in enumerate(sources(t)):
             site = site_ref[pl.ds(s, 1), :]
             kx = (site * 43691) >> 23
             lanes = pl.ds(pl.multiple_of(t * 256 + h * 128, 128), 128)
             picks_x[:, lanes] = folded(kx)
             picks_y[:, lanes] = folded(site - kx * 192)
+
+    pick(0)
+    pick(1)
+    relayed(1)
+    for k in range(2, 7):
+        relay(k)
+        pick(k)
+        if k == 2:
+            pick(7)
+        relayed(k)
 
     recv_b[pl.ds(me, 1)] = send_b[pl.ds(me, 1)]
     cols_b[1]()
@@ -449,6 +470,7 @@
             scratch(32, 2, 128),
             pltpu.SemaphoreType.DMA((22,)),
             pltpu.SemaphoreType.DMA((8,)),
+            pltpu.SemaphoreType.REGULAR((14,)),
         ],
         compiler_params=pltpu.CompilerParams(
             collective_id=0, has_side_effects=True, vmem_limit_bytes=60000000

time: 48.3 us -> 52.2 us (1.081)
  Pallas kernels: 47.6 us -> 51.5 us
    pallas_call x1, Pallas kernels: 47.6 us -> 51.5 us  [on_device(): pl.pallas_call(kernel, out_shape=pltpu.VMEM((16, 4, GRID), F32), in_specs...]
where the time goes in v5:
time: 52.2 us; the launch traced here: 52.1 us
  Pallas kernels  51.5 us (99%)
  local copies, waits for them, and re-layouts  0.63 us (1%)
    pallas_call x1, Pallas kernels, on_device(): pl.pallas_call(kernel, out_shape=pltpu.VMEM((16, 4, GRID), F32), in_specs...  51.5 us

profile of v5, /device:TPU:1, one launch (start us, length us, event | category | flops | bytes accessed | tf_op | source)
XLA Modules:
  0.0 52.1 jit_solution(7546143220844205530)
XLA Ops:
  0.0 51.5 %shard_map.91 = f32[16,4,192]{2,1,0:T(4,128)S(1)} custom-call(s32[64]{0:T(128)} %count_ref.1, s32[16,128]{1,0:T(8,128)} %bitcast.10, s32[4,128]{1,0:T(4,128)} %bitcast.11, bf16[16,4,192]{2,1,0:T(4,128)(2,1)} %bitcast.9, bf16[1536,512]{1,0:T(8,128)(2,1)} %bitcast.8, f32[3,192,192]{2,1,0:T(8,128)} %pot_hbm.1, f32[512,512]{1,0:T(8,128)} %coup_hbm.1, ...), custom_call_target="tpu_custom_call" | custom-call | tf_op jit(solution)/shard_map/pallas_call | solution.py:432
  51.5 0.6 %copy.11 = f32[8,2,4,192]{3,2,1,0:T(4,128)} copy(f32[8,2,4,192]{3,2,1,0:T(4,128)S(1)} %bitcast.7) | data formatting | bytes 98304

commit v6 on v4

--- a/solution.py
+++ b/solution.py
@@ -64,7 +64,7 @@
     site_ref, atom_ref, orb_ref, proj_ref, pot_ref, coup_ref, plane_ref, ztab_ref,
     wide, send_b, recv_b, send_pb, recv_pb, turn, stage, send_z, recv_z, send_pz, recv_pz,
     picks_x, picks_y, weights, grid_sum, grid_back, coupled_h, coupled_l, found, back_z, got_z,
-    back_b, got_b, back_pb, got_pb, sems, load_sems,
+    back_b, got_b, back_pb, got_pb, sems, load_sems, relays,
 ):
     block = lax.axis_index("ga")
     band = lax.axis_index("band")
@@ -143,10 +143,20 @@
     orb_in.start()
     ztab_in.start()
 
-    for d in FAR_FIRST[ZN]:
+    for d in (4, ZN - 4, 3, ZN - 3):
         pl.semaphore_signal(barrier, inc=1, device_id=on_z(d)[0], device_id_type=MESH)
     for d in FAR_FIRST[peers]:
         pl.semaphore_signal(barrier, inc=1, device_id=on_plane(d)[0], device_id_type=MESH)
+    for d in (2, ZN - 2, 1, ZN - 1):
+        pl.semaphore_signal(barrier, inc=1, device_id=on_z(d)[0], device_id_type=MESH)
+
+    def relay():
+        for side, d in enumerate((4, ZN - 4)):
+            pl.semaphore_signal(relays.at[side], inc=1, device_id=on_z(d)[0], device_id_type=MESH)
+
+    def relayed():
+        for side in range(2):
+            pl.semaphore_wait(relays.at[side], 1)
 
     for load in loads[2:]:
         load.start()
@@ -182,6 +192,10 @@
         for n in range(8):
             send_b[8 * x + n] = along_z[4 * n : 4 * n + 4, 128 * x : 128 * x + 128].astype(BF16)
 
+    pl.semaphore_wait(barrier, peers + 7)
+    relay()
+    cols_b[0]()
+
     def slot_rows(slot, starts):
         parts = [wide_rows(pl.ds(start + slot, 8, stride=4)) for start in starts]
         return jnp.concatenate(parts, axis=0).astype(BF16)
@@ -194,9 +208,6 @@
     for x in range(XN):
         for c in range(2):
             send_pb[8 * x : 8 * x + 8, c, :] = partial[8 * c : 8 * c + 8, 128 * x : 128 * x + 128]
-
-    pl.semaphore_wait(barrier, ZN + peers - 2)
-    cols_b[0]()
     proj_b[0]()
 
     stage[...] = jnp.zeros_like(stage)
@@ -234,6 +245,7 @@
         for zi in range(3):
             stage[pl.ds(c * 3 + zi, 16, stride=8), :] = turned[64 * c + 16 * zi : 64 * c + 16 * zi + 16]
     send_z[...] = stage[...].reshape(16, 8, 128).astype(BF16)
+    relayed()
     cols_z_start()
     recv_z[pl.ds(zz, 1)] = send_z[pl.ds(zz, 1)]
 
@@ -449,6 +461,7 @@
             scratch(32, 2, 128),
             pltpu.SemaphoreType.DMA((22,)),
             pltpu.SemaphoreType.DMA((8,)),
+            pltpu.SemaphoreType.REGULAR((2,)),
         ],
         compiler_params=pltpu.CompilerParams(
             collective_id=0, has_side_effects=True, vmem_limit_bytes=60000000

time: 48.3 us -> 46.1 us (0.954)
  Pallas kernels: 47.6 us -> 45.3 us
    pallas_call x1, Pallas kernels: 47.6 us -> 45.3 us  [on_device(): pl.pallas_call(kernel, out_shape=pltpu.VMEM((16, 4, GRID), F32), in_specs...]
where the time goes in v6:
time: 46.1 us; the launch traced here: 46 us
  Pallas kernels  45.3 us (98%)
  local copies, waits for them, and re-layouts  0.63 us (1%)
    pallas_call x1, Pallas kernels, on_device(): pl.pallas_call(kernel, out_shape=pltpu.VMEM((16, 4, GRID), F32), in_specs...  45.3 us

profile of v6, /device:TPU:1, one launch (start us, length us, event | category | flops | bytes accessed | tf_op | source)
XLA Modules:
  0.0 46.0 jit_solution(10853285638016974030)
XLA Ops:
  0.0 45.3 %shard_map.91 = f32[16,4,192]{2,1,0:T(4,128)S(1)} custom-call(s32[64]{0:T(128)} %count_ref.1, s32[16,128]{1,0:T(8,128)} %bitcast.10, s32[4,128]{1,0:T(4,128)} %bitcast.11, bf16[16,4,192]{2,1,0:T(4,128)(2,1)} %bitcast.9, bf16[1536,512]{1,0:T(8,128)(2,1)} %bitcast.8, f32[3,192,192]{2,1,0:T(8,128)} %pot_hbm.1, f32[512,512]{1,0:T(8,128)} %coup_hbm.1, ...), custom_call_target="tpu_custom_call" | custom-call | tf_op jit(solution)/shard_map/pallas_call | solution.py:423
  45.3 0.6 %copy.11 = f32[8,2,4,192]{3,2,1,0:T(4,128)} copy(f32[8,2,4,192]{3,2,1,0:T(4,128)S(1)} %bitcast.7) | data formatting | bytes 98304
